TPU v7x, 32 devices: a whole 2x2x4 slice. The times are simulated.
32 devices in a mesh: tm: 16 (over z, x, core), space: 2 (over y).
Axes of the slice: x: 2, y: 2, z: 4, core: 2. Of those that a mesh axis runs over, the one named last changes fastest.
Arguments:
- snapshots: bfloat16 [512, 5, 4096], P('tm', None, 'space'), may hold values from -210 to 210, as said below
- basis: bfloat16 [2, 33, 16, 5, 4096], P(None, None, None, None, ('space', 'tm')), may hold values from -6 to 6
- mass_table: float32 [8, 64, 64], replicated, may hold values from -0.03 to 3, as said below
- elem_kind: int32 [64], P(('space', 'tm')), may hold values from 0 to 7
- offsets: int32 [8], replicated, may hold values from 0 to 256, as said below
Outputs:
- coeffs: float32 [2, 33, 8, 16], replicated
- new_basis: bfloat16 [2, 33, 16, 5, 4096], P(None, None, None, None, ('space', 'tm'))
Inputs may be any that keep to these rules, and one draw needn't show every extreme that they name: `snapshots`: rows of flow data. `mass_table`: each block is symmetric and positive definite. `offsets`: some block starts at 0 and some at 256.
All inputs are finite; a program needn't handle non-finite values.
Results may differ from a plain program's by a relative error of at most 0.0095.
Values may be sent and summed in bfloat16 or wider, within the bound.
A program may use at most 64 MiB of HBM per device.

v0:
```python
import functools
import math

import jax
import jax.numpy as jnp
from jax import lax
from jax.experimental import pallas as pl
from jax.experimental.pallas import tpu as pltpu
from jax.sharding import PartitionSpec as P

NT = 256
GROUP = 8
MESH = pl.DeviceIdType.MESH
BF = jnp.bfloat16
F32 = jnp.float32


def mm(a, b, contract):
    return lax.dot_general(a, b, (contract, ((), ())), preferred_element_type=F32)


def kernel(
    n_tm, n_sp, low, entries, chunks,
    snap, basis, mass_in, kinds_in, offs_in,
    sh, y_out,
    table, ub, xb, line, plane, yb, mass, kinds, offs, *rest,
):
    recs, (a_send, a_recv, l_sem, s1, r1, s2, r2, s3, r3) = rest[: len(chunks)], rest[len(chunks) :]
    tm = lax.axis_index("tm")
    sp = lax.axis_index("space")
    high = n_tm // low
    side = low * n_sp
    mid = n_tm // 2
    turn = lax.rem(tm + n_tm - n_tm // 4, n_tm)
    spot = lax.div(turn, mid) * (side // 2) + sp * mid + lax.rem(turn, mid)
    level = lax.div(tm, low)
    freqs = basis.shape[1]
    rows, pts = recs[0].shape[2:]
    groups = sh.shape[0] // (2 * GROUP * 8)
    record = n_tm * rows
    blocks = offs.shape[0]
    modes = basis.shape[3]
    upo = plane.shape[1]
    owners = xb.shape[0] // upo
    half = GROUP * blocks
    lanes = GROUP * modes

    def beside(p):
        r = lax.rem(p, side // 2)
        back = lax.div(p, side // 2) * mid + lax.rem(r, mid)
        return {"tm": lax.rem(back + n_tm // 4, n_tm), "space": lax.div(r, mid)}

    barrier = pltpu.get_barrier_semaphore()

    def greet_line(i, carry):
        pl.semaphore_signal(
            barrier, inc=1, device_id={"tm": lax.rem(tm + i, n_tm), "space": sp}, device_id_type=MESH
        )
        return carry

    def greet_side(i, carry):
        to = lax.rem(sp + lax.div(i, low), n_sp)
        pl.semaphore_signal(
            barrier, inc=1, device_id={"tm": level * low + lax.rem(i, low), "space": to}, device_id_type=MESH
        )
        return carry

    lax.fori_loop(1, n_tm, greet_line, 0, unroll=side <= 32)
    lax.fori_loop(low, side, greet_side, 0, unroll=side <= 32)
    loads = [
        pltpu.make_async_copy(offs_in, offs, l_sem.at[0]),
        pltpu.make_async_copy(kinds_in, kinds, l_sem.at[1]),
        pltpu.make_async_copy(mass_in, mass, l_sem.at[2]),
        pltpu.make_async_copy(basis, ub.at[:, pl.ds(0, freqs)], l_sem.at[3]),
    ]
    for cp in loads:
        cp.start()
    pl.semaphore_wait(barrier, n_tm - 1 + side - low)

    for ci, (v0, v1) in enumerate(chunks):

        def block(to):
            return snap.at[pl.ds(v0, v1 - v0), :, pl.ds(pl.multiple_of(to * pts, pts), pts)]

        def send(i, carry):
            d = lax.div(i + 1, 2)
            to = lax.rem(tm + n_tm // 2 + jnp.where(lax.rem(i, 2) == 0, d, -d) + n_tm, n_tm)
            pltpu.make_async_remote_copy(
                block(to), recs[ci].at[tm], a_send.at[ci], a_recv.at[ci],
                device_id={"tm": to, "space": sp}, device_id_type=MESH,
            ).start()
            return carry

        lax.fori_loop(0, n_tm - 1, send, 0, unroll=side <= 32)
        pltpu.make_async_copy(block(tm), recs[ci].at[tm], a_recv.at[ci]).start()

    loads[0].wait()
    row = lax.broadcasted_iota(jnp.int32, (blocks, record), 0)
    lag = lax.broadcasted_iota(jnp.int32, (blocks, record), 1)
    for b in range(blocks):
        lag = jnp.where(row == b, lag - offs[b], lag)
    inside = (lag >= 0) & (lag < NT)
    theta = jnp.clip(lag, 0, NT - 1).astype(F32) * (2.0 * math.pi / NT)
    c1, s1v = jnp.cos(theta), jnp.sin(theta)
    win = jnp.where(inside, (0.5 - 0.5 * c1) * (1.0 / math.sqrt(0.375 * NT)), 0.0)
    cc, ss = win, jnp.zeros_like(win)
    for f in range(0, groups * GROUP, 2):
        c_next, s_next = cc * c1 - ss * s1v, ss * c1 + cc * s1v
        at = (f // GROUP) * 2 * half + (f % GROUP) * blocks
        table[at : at + 2 * blocks] = jnp.concatenate([cc, c_next], axis=0).astype(BF)
        table[at + half : at + half + 2 * blocks] = jnp.concatenate([-ss, -s_next], axis=0).astype(BF)
        cc, ss = c_next * c1 - s_next * s1v, s_next * c1 + c_next * s1v

    loads[1].wait()
    loads[2].wait()
    size = mass.shape[1]
    elems = pts // size
    strips = []
    for e in range(elems):
        kind = jnp.full((size, size), kinds[e], jnp.int32)
        blk = mass[0]
        for k in range(1, mass.shape[0]):
            blk = jnp.where(kind == k, mass[k], blk)
        zero = jnp.zeros_like(blk)
        strips.append(jnp.concatenate([blk if j == e else zero for j in range(elems)], axis=1))
    m_all = jnp.concatenate(strips, axis=0)
    m_hi = m_all.astype(BF)
    m_lo = (m_all - m_hi.astype(F32)).astype(BF)
    m_stack = jnp.concatenate([m_hi, m_hi, m_lo], axis=0)

    loads[3].wait()
    ub[:, freqs:] = jnp.zeros((2, groups * GROUP - freqs) + ub.shape[2:], BF)

    row_f = lax.broadcasted_iota(jnp.int32, (GROUP, blocks, lanes), 0)
    lane = lax.broadcasted_iota(jnp.int32, (GROUP, blocks, lanes), 2)
    diag_k = row_f == lane // modes
    diag_b = row_f == (lane % half) // blocks
    lane2 = lax.broadcasted_iota(jnp.int32, (blocks, lanes), 1)

    def fold(full, mask):
        return jnp.sum(jnp.where(mask, full.reshape(GROUP, blocks, lanes), 0.0), axis=0)

    total = [None] * (3 * groups)
    for ci, (v0, v1) in enumerate(chunks):
        rec = recs[ci]
        pltpu.make_async_copy(rec, rec, a_recv.at[ci]).wait()
        count = v1 - v0
        x = jnp.concatenate([rec[:, v].reshape(record, pts) for v in range(count)], axis=1)
        spec = mm(table[...], x, ((1,), (0,)))
        s_hi = spec.astype(BF)
        s_lo = (spec - s_hi.astype(F32)).astype(BF)
        sh[:, v0 * pts : v1 * pts] = s_hi
        wts = []
        for v in range(count):
            cut = slice(v * pts, (v + 1) * pts)
            lhs = jnp.concatenate([s_hi[:, cut], s_lo[:, cut], s_hi[:, cut]], axis=1)
            wts.append(mm(lhs, m_stack, ((1,), (0,))).astype(BF))
        wt = jnp.concatenate(wts, axis=1)
        for g in range(groups):
            top = g * 2 * half
            f0 = g * GROUP
            u = [
                jnp.concatenate(
                    [ub[c, f0 : f0 + GROUP, v].reshape(lanes, pts) for v in range(v0, v1)], axis=1
                )
                for c in range(2)
            ]
            lhs = jnp.concatenate(u + [s_hi[top : top + 2 * half]], axis=0)
            full = mm(wt[top : top + 2 * half], lhs, ((1,), (1,)))
            rr = fold(full[:half, :lanes], diag_k)
            ri = fold(full[:half, lanes : 2 * lanes], diag_k)
            ir = fold(full[half:, :lanes], diag_k)
            ii = fold(full[half:, lanes : 2 * lanes], diag_k)
            p_r = fold(full[:half, 2 * lanes :], diag_b)
            p_i = pltpu.roll(fold(full[half:, 2 * lanes :], diag_b), half, 1)
            new = [rr + ii, ir - ri, jnp.where(lane2 < half, p_r + p_i, p_i - p_r)]
            for j in range(3):
                at = 3 * g + j
                total[at] = new[j] if ci == 0 else total[at] + new[j]
    for at in range(3 * groups):
        xb[at] = total[at]

    mine = pl.ds(spot * upo, upo)

    def scatter(i, carry):
        o = lax.rem(spot + i, owners)

        @pl.when(o != spot)
        def _():
            pltpu.make_async_remote_copy(
                xb.at[pl.ds(o * upo, upo)], plane.at[spot], s1, r1,
                device_id=beside(o), device_id_type=MESH,
            ).start()

        return carry

    lax.fori_loop(0, owners, scatter, 0, unroll=side <= 32)

    def wait_bytes(ref, sem):
        pltpu.make_async_copy(ref, ref, sem).wait()

    @pl.when(spot < owners)
    def _():
        plane[spot] = xb[mine]
        wait_bytes(plane.at[pl.ds(0, side - 1)], r1)
        line[level] = jnp.sum(plane[...], axis=0)

        def exchange(i, carry):
            to = lax.rem(level + i, high) * low + lax.rem(tm, low)
            pltpu.make_async_remote_copy(
                line.at[level], line.at[level], s2, r2,
                device_id={"tm": to, "space": sp}, device_id_type=MESH,
            ).start()
            return carry

        if high > 1:
            lax.fori_loop(1, high, exchange, 0)
            wait_bytes(line.at[pl.ds(0, high - 1)], r2)
        yb[mine] = jnp.sum(line[...], axis=0)

        def gather(i, carry):
            pltpu.make_async_remote_copy(
                yb.at[mine], yb.at[mine], s3, r3,
                device_id=beside(lax.rem(spot + i, side)), device_id_type=MESH,
            ).start()
            return carry

        lax.fori_loop(1, side, gather, 0, unroll=side <= 32)
        wait_bytes(yb.at[pl.ds(0, (owners - 1) * upo)], r3)

    @pl.when(spot >= owners)
    def _():
        wait_bytes(yb, r3)

    y_out[...] = yb[...]
    for ci in range(len(chunks)):
        wait_bytes(recs[ci].at[pl.ds(0, n_tm - 1)], a_send.at[ci])

    @pl.when(spot < owners)
    def _():
        wait_bytes(xb.at[pl.ds(0, (owners - 1) * upo)], s1)
        if high > 1:
            wait_bytes(line.at[pl.ds(0, high - 1)], s2)
        wait_bytes(plane.at[pl.ds(0, side - 1)], s3)

    @pl.when(spot >= owners)
    def _():
        wait_bytes(xb, s1)


def finish(entries, yb, sh, coef_out, new_out, ob, o_sem):
    freqs, nvar, modes, pts = new_out.shape[1:]
    blocks = coef_out.shape[1]
    half = GROUP * blocks
    lanes = GROUP * modes
    groups = -(-freqs // GROUP)
    row_f = lax.broadcasted_iota(jnp.int32, (GROUP, blocks, lanes), 0)
    lane = lax.broadcasted_iota(jnp.int32, (GROUP, blocks, lanes), 2)
    diag_k = row_f == lane // modes
    diag_b = row_f == (lane % half) // blocks
    lane2 = lax.broadcasted_iota(jnp.int32, (blocks, lanes), 1)
    scale = 1.0 / math.sqrt(entries)

    def spread_rows(val, mask):
        big = jnp.broadcast_to(val[None], (GROUP, blocks, lanes))
        return jnp.where(mask, big, 0.0).reshape(half, lanes)

    copies, held = [], []
    for g in range(groups):
        top = g * 2 * half
        f0 = g * GROUP
        nf = min(GROUP, freqs - f0)
        co = [yb[3 * g + c] * scale for c in range(2)]
        held.append(co)
        cr, ci = [v.astype(BF).astype(F32) for v in co]
        gram = yb[3 * g + 2]
        d_r, d_i = spread_rows(cr, diag_k), spread_rows(ci, diag_k)
        turned = pltpu.roll(gram, half, 1)
        turned = jnp.where(lane2 < half, -turned, turned)
        quad = jnp.concatenate([spread_rows(gram, diag_b), spread_rows(turned, diag_b)], axis=0)
        vec = jnp.concatenate([d_r, d_i], axis=0)
        energy = jnp.sum(vec * mm(quad.astype(BF), vec.astype(BF), ((1,), (0,))), axis=0, keepdims=True)
        factor = 1.0 / jnp.sqrt(energy / entries + 1e-06)
        fac = jnp.transpose(jnp.broadcast_to(factor, (pts, lanes)))
        s_g = sh[top : top + 2 * half]
        for c in range(2):
            d = jnp.concatenate([d_r, -d_i] if c == 0 else [d_i, d_r], axis=0)
            field = mm(jnp.transpose(d).astype(BF), s_g, ((1,), (0,)))
            for v in range(nvar):
                val = (field[:, v * pts : (v + 1) * pts] * fac).astype(BF).reshape(GROUP, modes, pts)
                ob[c, f0 : f0 + nf, v] = val[:nf]
        cp = pltpu.make_async_copy(ob.at[:, pl.ds(f0, nf)], new_out.at[:, pl.ds(f0, nf)], o_sem.at[g])
        cp.start()
        copies.append(cp)

    mode_row = lax.broadcasted_iota(jnp.int32, (blocks, modes, lanes), 1)
    pick = mode_row == lax.broadcasted_iota(jnp.int32, (blocks, modes, lanes), 2) % modes
    e_row = lax.broadcasted_iota(jnp.int32, (lanes, freqs), 0) // modes
    e_col = lax.broadcasted_iota(jnp.int32, (lanes, freqs), 1)
    moves = [jnp.where(e_col == e_row + g * GROUP, 1.0, 0.0).astype(BF) for g in range(groups)]
    move = jnp.concatenate(moves + moves, axis=0)
    for c in range(2):
        his, los = [], []
        for g in range(groups):
            val = held[g][c]
            if g == groups - 1:
                val = jnp.where(lane2 < (freqs - g * GROUP) * modes, val, 0.0)
            hi = val.astype(BF).astype(F32)
            for part, to in ((hi, his), (val - hi, los)):
                big = jnp.broadcast_to(part[:, None, :], (blocks, modes, lanes))
                to.append(jnp.where(pick, big, 0.0).reshape(blocks * modes, lanes).astype(BF))
        moved = mm(jnp.concatenate(his + los, axis=1), move, ((1,), (0,)))
        coef_out[c] = moved.reshape(blocks, modes, freqs)
    for cp in copies:
        cp.wait()


def solution(mesh):
    n_tm, n_sp = mesh.shape["tm"], mesh.shape["space"]
    n = n_tm * n_sp

    def on_device(snapshots, basis, mass_table, elem_kind, offsets):
        rows, nvar, slab = snapshots.shape
        _, freqs, modes, _, pts = basis.shape
        blocks = offsets.shape[0]
        groups = -(-freqs // GROUP)
        entries = nvar * pts * n
        units = 3 * groups
        low = n_tm
        side = low * n_sp
        upo = -(-units // side)
        owners = -(-units // upo)
        table_rows = groups * 2 * GROUP * blocks
        unit = (blocks, GROUP * modes)
        chunks = tuple((v, min(v + 2, nvar)) for v in range(0, nvar, 2))
        snap = jnp.transpose(snapshots, (1, 0, 2))
        base = jnp.transpose(basis, (0, 1, 3, 2, 4))
        hbm = pl.BlockSpec(memory_space=pltpu.HBM)
        vmem = pl.BlockSpec(memory_space=pltpu.VMEM)
        spec, total = pl.pallas_call(
            functools.partial(kernel, n_tm, n_sp, low, entries, chunks),
            out_shape=(
                jax.ShapeDtypeStruct((table_rows, nvar * pts), BF),
                jax.ShapeDtypeStruct((owners * upo,) + unit, F32),
            ),
            in_specs=[hbm] * 5,
            out_specs=(vmem, vmem),
            scratch_shapes=[
                pltpu.VMEM((table_rows, rows * n_tm), BF),
                pltpu.VMEM((2, groups * GROUP, nvar, modes, pts), BF),
                pltpu.VMEM((owners * upo,) + unit, F32),
                pltpu.VMEM((n_tm // low, upo) + unit, F32),
                pltpu.VMEM((side, upo) + unit, F32),
                pltpu.VMEM((owners * upo,) + unit, F32),
                pltpu.VMEM(mass_table.shape, F32),
                pltpu.SMEM(elem_kind.shape, jnp.int32),
                pltpu.SMEM(offsets.shape, jnp.int32),
            ]
            + [pltpu.VMEM((n_tm, v1 - v0, rows, pts), BF) for v0, v1 in chunks]
            + [
                pltpu.SemaphoreType.DMA((len(chunks),)),
                pltpu.SemaphoreType.DMA((len(chunks),)),
                pltpu.SemaphoreType.DMA((4,)),
            ]
            + [pltpu.SemaphoreType.DMA] * 6,
            compiler_params=pltpu.CompilerParams(
                collective_id=0, has_side_effects=True, vmem_limit_bytes=48 * 1024 * 1024
            ),
        )(*[pltpu.with_memory_space_constraint(a, pltpu.HBM) for a in (snap, base, mass_table, elem_kind, offsets)])
        coef, new = pl.pallas_call(
            functools.partial(finish, entries),
            out_shape=(
                jax.ShapeDtypeStruct((2, blocks, modes, freqs), F32),
                jax.ShapeDtypeStruct(base.shape, BF),
            ),
            in_specs=[vmem, vmem],
            out_specs=(vmem, hbm),
            scratch_shapes=[pltpu.VMEM(base.shape, BF), pltpu.SemaphoreType.DMA((groups,))],
            compiler_params=pltpu.CompilerParams(vmem_limit_bytes=32 * 1024 * 1024),
        )(total, spec)
        return jnp.transpose(coef, (0, 3, 1, 2)), jnp.transpose(new, (0, 1, 3, 2, 4))

    return jax.shard_map(
        on_device,
        mesh=mesh,
        in_specs=(
            P("tm", None, "space"),
            P(None, None, None, None, ("space", "tm")),
            P(),
            P(("space", "tm")),
            P(),
        ),
        out_specs=(P(), P(None, None, None, None, ("space", "tm"))),
        check_vma=False,
    )
```

profile of v0, /device:TPU:0, one launch (start us, length us, event | category | flops | bytes accessed | tf_op | source)
XLA Modules:
  0.0 35.2 jit_solution(7653104731778670101)
XLA Ops:
  0.6 32.5 %shard_map.68 = (bf16[640,640]{1,0:T(8,128)(2,1)S(1)}, f32[15,8,128]{2,1,0:T(8,128)S(1)}) custom-call(bf16[5,32,2048]{2,1,0:T(8,128)(2,1)} %bitcast.5, bf16[2,33,5,16,128]{4,3,2,1,0:T(8,128)(2,1)} %bitcast.4, f32[8,64,64]{2,1,0:T(8,128)} %mass_in.1, s32[2]{0:T(128)} %kinds_in.1, s32[8]{0:T(128)} %offs_in.1), custom_call_target="tpu_custom_call" | custom-call | tf_op jit(solution)/shard_map/pallas_call | solution.py:340
  33.1 2.1 %shard_map.69 = (f32[2,8,16,33]{3,2,1,0:T(8,128)}, bf16[2,33,5,16,128]{4,3,2,1,0:T(8,128)(2,1)}) custom-call(f32[15,8,128]{2,1,0:T(8,128)S(1)} %get-tuple-element.6.yb, bf16[640,640]{1,0:T(8,128)(2,1)S(1)} %get-tuple-element.7.sh), custom_call_target="tpu_custom_call" | custom-call | tf_op jit(solution)/shard_map/pallas_call | solution.py:370
where the time goes:
time: 35.4 us; the launch traced here: 35.2 us
  Pallas kernels  34.6 us (98%)
  between operations  0.64 us (2%)
    pallas_call x1, Pallas kernels, on_device(): pl.pallas_call(functools.partial(kernel, n_tm, n_sp, low, entries, chunks...  32.5 us
    pallas_call x1, Pallas kernels, on_device(): pl.pallas_call(functools.partial(finish, entries), out_shape=(jax.ShapeDt...  2.14 us

commit v1 on v0

--- a/solution.py
+++ b/solution.py
@@ -10,6 +10,7 @@
 
 NT = 256
 GROUP = 8
+LEVELS = 4
 MESH = pl.DeviceIdType.MESH
 BF = jnp.bfloat16
 F32 = jnp.float32
@@ -25,10 +26,14 @@
     sh, y_out,
     table, ub, xb, line, plane, yb, mass, kinds, offs, *rest,
 ):
-    recs, (a_send, a_recv, l_sem, s1, r1, s2, r2, s3, r3) = rest[: len(chunks)], rest[len(chunks) :]
+    recs, (a_send, a_recv, l_sem, known, s1, r1, s2, r2, s3, r3) = rest[: len(chunks)], rest[len(chunks) :]
     tm = lax.axis_index("tm")
     sp = lax.axis_index("space")
     high = n_tm // low
+    quart = n_tm // LEVELS
+    lev, place = lax.div(tm, quart), lax.rem(tm, quart)
+    edge = (lev == 0) | (lev == LEVELS - 1)
+    inward = jnp.where(lev < LEVELS // 2, 1, -1)
     side = low * n_sp
     mid = n_tm // 2
     turn = lax.rem(tm + n_tm - n_tm // 4, n_tm)
@@ -52,21 +57,27 @@
 
     barrier = pltpu.get_barrier_semaphore()
 
-    def greet_line(i, carry):
+    def signal(sem, to_tm, to_sp):
         pl.semaphore_signal(
-            barrier, inc=1, device_id={"tm": lax.rem(tm + i, n_tm), "space": sp}, device_id_type=MESH
+            sem, inc=1, device_id={"tm": to_tm, "space": to_sp}, device_id_type=MESH
         )
+
+    for dl in (1, -1, 0):
+
+        def greet(i, carry):
+            to = (lev + dl) * quart + lax.rem(place + i, quart)
+            signal(barrier, to, sp)
+            return carry
+
+        @pl.when((lev + dl >= 0) & (lev + dl < LEVELS))
+        def _():
+            lax.fori_loop(1 if dl == 0 else 0, quart, greet, 0, unroll=side <= 32)
+
+    def greet_side(i, carry):
+        signal(barrier, tm, lax.rem(sp + i, n_sp))
         return carry
 
-    def greet_side(i, carry):
-        to = lax.rem(sp + lax.div(i, low), n_sp)
-        pl.semaphore_signal(
-            barrier, inc=1, device_id={"tm": level * low + lax.rem(i, low), "space": to}, device_id_type=MESH
-        )
-        return carry
-
-    lax.fori_loop(1, n_tm, greet_line, 0, unroll=side <= 32)
-    lax.fori_loop(low, side, greet_side, 0, unroll=side <= 32)
+    lax.fori_loop(1, n_sp, greet_side, 0, unroll=side <= 32)
     loads = [
         pltpu.make_async_copy(offs_in, offs, l_sem.at[0]),
         pltpu.make_async_copy(kinds_in, kinds, l_sem.at[1]),
@@ -75,24 +86,63 @@
     ]
     for cp in loads:
         cp.start()
-    pl.semaphore_wait(barrier, n_tm - 1 + side - low)
-
-    for ci, (v0, v1) in enumerate(chunks):
-
-        def block(to):
-            return snap.at[pl.ds(v0, v1 - v0), :, pl.ds(pl.multiple_of(to * pts, pts), pts)]
+    near = jnp.where(edge, 2, 3)
+    pl.semaphore_wait(barrier, near * quart - 1 + n_sp - 1)
+
+    def relay(stage):
+        for dl in (1, -1):
+            seen = lev - dl * (stage - 1)
+
+            @pl.when((seen >= 0) & (seen < LEVELS) & (lev + dl >= 0) & (lev + dl < LEVELS))
+            def _():
+                signal(known.at[stage - 2], tm + dl * quart, sp)
+
+    def learn(stage):
+        for dl in (1, -1):
+
+            @pl.when((lev + dl * stage >= 0) & (lev + dl * stage < LEVELS))
+            def _():
+                pl.semaphore_wait(known.at[stage - 2], 1)
+
+    def send_level(ci, to_lev, first=0):
+        v0, v1 = chunks[ci]
 
         def send(i, carry):
-            d = lax.div(i + 1, 2)
-            to = lax.rem(tm + n_tm // 2 + jnp.where(lax.rem(i, 2) == 0, d, -d) + n_tm, n_tm)
+            to = to_lev * quart + lax.rem(place + i, quart)
             pltpu.make_async_remote_copy(
-                block(to), recs[ci].at[tm], a_send.at[ci], a_recv.at[ci],
+                snap.at[pl.ds(v0, v1 - v0), :, pl.ds(pl.multiple_of(to * pts, pts), pts)],
+                recs[ci].at[tm], a_send.at[ci], a_recv.at[ci],
                 device_id={"tm": to, "space": sp}, device_id_type=MESH,
             ).start()
             return carry
 
-        lax.fori_loop(0, n_tm - 1, send, 0, unroll=side <= 32)
-        pltpu.make_async_copy(block(tm), recs[ci].at[tm], a_recv.at[ci]).start()
+        lax.fori_loop(first, quart, send, 0, unroll=side <= 32)
+
+    relay(2)
+    for ci, (v0, v1) in enumerate(chunks):
+        mine = snap.at[pl.ds(v0, v1 - v0), :, pl.ds(pl.multiple_of(tm * pts, pts), pts)]
+        if ci == 0:
+            send_level(ci, lev + inward)
+            pl.when(jnp.logical_not(edge))(lambda: send_level(ci, lev - inward))
+            send_level(ci, lev, 1)
+            learn(2)
+            relay(3)
+            send_level(ci, lev + 2 * inward)
+            learn(3)
+            pl.when(edge)(lambda: send_level(ci, lev + 3 * inward))
+
+            def tell(i, carry):
+                signal(known.at[2], tm, lax.rem(sp + i, n_sp))
+                return carry
+
+            lax.fori_loop(1, n_sp, tell, 0, unroll=side <= 32)
+        else:
+            pl.when(edge)(lambda: send_level(ci, lev + 3 * inward))
+            send_level(ci, lev + 2 * inward)
+            send_level(ci, lev + inward)
+            pl.when(jnp.logical_not(edge))(lambda: send_level(ci, lev - inward))
+            send_level(ci, lev, 1)
+        pltpu.make_async_copy(mine, recs[ci].at[tm], a_recv.at[ci]).start()
 
     loads[0].wait()
     row = lax.broadcasted_iota(jnp.int32, (blocks, record), 0)
@@ -181,6 +231,7 @@
         xb[at] = total[at]
 
     mine = pl.ds(spot * upo, upo)
+    pl.semaphore_wait(known.at[2], n_sp - 1)
 
     def scatter(i, carry):
         o = lax.rem(spot + i, owners)
@@ -361,6 +412,7 @@
                 pltpu.SemaphoreType.DMA((len(chunks),)),
                 pltpu.SemaphoreType.DMA((len(chunks),)),
                 pltpu.SemaphoreType.DMA((4,)),
+                pltpu.SemaphoreType.REGULAR((3,)),
             ]
             + [pltpu.SemaphoreType.DMA] * 6,
             compiler_params=pltpu.CompilerParams(

time: 35.4 us -> 34.3 us (0.969)
  Pallas kernels: 34.6 us -> 33.5 us
    pallas_call x1, Pallas kernels: 32.5 us -> 31.3 us  [on_device(): pl.pallas_call(functools.partial(kernel, n_tm, n_sp, low, entries, chunks...]
where the time goes in v1:
time: 34.3 us; the launch traced here: 34.1 us
  Pallas kernels  33.5 us (98%)
  between operations  0.64 us (2%)
    pallas_call x1, Pallas kernels, on_device(): pl.pallas_call(functools.partial(kernel, n_tm, n_sp, low, entries, chunks...  31.3 us
    pallas_call x1, Pallas kernels, on_device(): pl.pallas_call(functools.partial(finish, entries), out_shape=(jax.ShapeDt...  2.14 us

profile of v1, /device:TPU:0, one launch (start us, length us, event | category | flops | bytes accessed | tf_op | source)
XLA Modules:
  0.0 34.1 jit_solution(11946051632599210973)
XLA Ops:
  0.6 31.3 %shard_map.68 = (bf16[640,640]{1,0:T(8,128)(2,1)S(1)}, f32[15,8,128]{2,1,0:T(8,128)S(1)}) custom-call(bf16[5,32,2048]{2,1,0:T(8,128)(2,1)} %bitcast.5, bf16[2,33,5,16,128]{4,3,2,1,0:T(8,128)(2,1)} %bitcast.4, f32[8,64,64]{2,1,0:T(8,128)} %mass_in.1, s32[2]{0:T(128)} %kinds_in.1, s32[8]{0:T(128)} %offs_in.1), custom_call_target="tpu_custom_call" | custom-call | tf_op jit(solution)/shard_map/pallas_call | solution.py:391
  32.0 2.1 %shard_map.69 = (f32[2,8,16,33]{3,2,1,0:T(8,128)}, bf16[2,33,5,16,128]{4,3,2,1,0:T(8,128)(2,1)}) custom-call(f32[15,8,128]{2,1,0:T(8,128)S(1)} %get-tuple-element.6.yb, bf16[640,640]{1,0:T(8,128)(2,1)S(1)} %get-tuple-element.7.sh), custom_call_target="tpu_custom_call" | custom-call | tf_op jit(solution)/shard_map/pallas_call | solution.py:422

commit v2 on v1

--- a/solution.py
+++ b/solution.py
@@ -16,29 +16,37 @@
 F32 = jnp.float32
 
 
+def owner_list(n_tm, n_sp, count):
+    quart = n_tm // LEVELS
+    first = [(quart, 0), (2 * quart, 0), (quart + 2, 0), (quart, 1)]
+    spots = [(t + c, s) for t, s in first for c in range(2)]
+    spots += [(t, s) for s in range(n_sp) for t in range(n_tm) if (t, s) not in spots]
+    return tuple(p for p in spots if p[0] < n_tm and p[1] < n_sp)[:count]
+
+
 def mm(a, b, contract):
     return lax.dot_general(a, b, (contract, ((), ())), preferred_element_type=F32)
 
 
 def kernel(
-    n_tm, n_sp, low, entries, chunks,
+    n_tm, n_sp, owners, entries, chunks,
     snap, basis, mass_in, kinds_in, offs_in,
     sh, y_out,
-    table, ub, xb, line, plane, yb, mass, kinds, offs, *rest,
+    table, ub, xb, plane, yb, mass, kinds, offs, *rest,
 ):
-    recs, (a_send, a_recv, l_sem, known, s1, r1, s2, r2, s3, r3) = rest[: len(chunks)], rest[len(chunks) :]
+    recs, (a_send, a_recv, l_sem, known, s1, r1, s2, r2) = rest[: len(chunks)], rest[len(chunks) :]
     tm = lax.axis_index("tm")
     sp = lax.axis_index("space")
-    high = n_tm // low
+    side = n_tm * n_sp
+    scale = 1.0 / math.sqrt(entries)
+    here = sp * n_tm + tm
+    is_own = [(tm == o_tm) & (sp == o_sp) for o_tm, o_sp in owners]
+    owner = functools.reduce(jnp.logical_or, is_own)
+    spot = sum(jnp.where(m, o, 0) for o, m in enumerate(is_own))
     quart = n_tm // LEVELS
     lev, place = lax.div(tm, quart), lax.rem(tm, quart)
     edge = (lev == 0) | (lev == LEVELS - 1)
     inward = jnp.where(lev < LEVELS // 2, 1, -1)
-    side = low * n_sp
-    mid = n_tm // 2
-    turn = lax.rem(tm + n_tm - n_tm // 4, n_tm)
-    spot = lax.div(turn, mid) * (side // 2) + sp * mid + lax.rem(turn, mid)
-    level = lax.div(tm, low)
     freqs = basis.shape[1]
     rows, pts = recs[0].shape[2:]
     groups = sh.shape[0] // (2 * GROUP * 8)
@@ -46,14 +54,8 @@
     blocks = offs.shape[0]
     modes = basis.shape[3]
     upo = plane.shape[1]
-    owners = xb.shape[0] // upo
     half = GROUP * blocks
     lanes = GROUP * modes
-
-    def beside(p):
-        r = lax.rem(p, side // 2)
-        back = lax.div(p, side // 2) * mid + lax.rem(r, mid)
-        return {"tm": lax.rem(back + n_tm // 4, n_tm), "space": lax.div(r, mid)}
 
     barrier = pltpu.get_barrier_semaphore()
 
@@ -223,78 +225,62 @@
             ii = fold(full[half:, lanes : 2 * lanes], diag_k)
             p_r = fold(full[:half, 2 * lanes :], diag_b)
             p_i = pltpu.roll(fold(full[half:, 2 * lanes :], diag_b), half, 1)
-            new = [rr + ii, ir - ri, jnp.where(lane2 < half, p_r + p_i, p_i - p_r)]
+            new = [(rr + ii) * scale, (ir - ri) * scale, jnp.where(lane2 < half, p_r + p_i, p_i - p_r)]
             for j in range(3):
                 at = 3 * g + j
                 total[at] = new[j] if ci == 0 else total[at] + new[j]
-    for at in range(3 * groups):
-        xb[at] = total[at]
-
-    mine = pl.ds(spot * upo, upo)
+    empty = jnp.zeros((blocks, lanes), F32)
+    total += [empty] * (2 * xb.shape[0] - len(total))
+    for at in range(xb.shape[0]):
+        xb[at] = jnp.concatenate(total[2 * at : 2 * at + 2], axis=0).astype(BF)
+
     pl.semaphore_wait(known.at[2], n_sp - 1)
-
-    def scatter(i, carry):
-        o = lax.rem(spot + i, owners)
-
-        @pl.when(o != spot)
+    for o, (o_tm, o_sp) in enumerate(owners):
+
+        @pl.when((tm != o_tm) | (sp != o_sp))
         def _():
             pltpu.make_async_remote_copy(
-                xb.at[pl.ds(o * upo, upo)], plane.at[spot], s1, r1,
-                device_id=beside(o), device_id_type=MESH,
+                xb.at[pl.ds(o * upo, upo)], plane.at[here], s1, r1,
+                device_id={"tm": o_tm, "space": o_sp}, device_id_type=MESH,
             ).start()
-
-        return carry
-
-    lax.fori_loop(0, owners, scatter, 0, unroll=side <= 32)
 
     def wait_bytes(ref, sem):
         pltpu.make_async_copy(ref, ref, sem).wait()
 
-    @pl.when(spot < owners)
+    @pl.when(owner)
     def _():
-        plane[spot] = xb[mine]
+        mine = pl.ds(spot * upo, upo)
+        plane[here] = xb[mine]
         wait_bytes(plane.at[pl.ds(0, side - 1)], r1)
-        line[level] = jnp.sum(plane[...], axis=0)
-
-        def exchange(i, carry):
-            to = lax.rem(level + i, high) * low + lax.rem(tm, low)
-            pltpu.make_async_remote_copy(
-                line.at[level], line.at[level], s2, r2,
-                device_id={"tm": to, "space": sp}, device_id_type=MESH,
-            ).start()
+        yb[mine] = jnp.sum(plane[...].astype(F32), axis=0).astype(BF)
+
+        def gather(i, carry):
+            @pl.when(i != tm * n_sp + sp)
+            def _():
+                pltpu.make_async_remote_copy(
+                    yb.at[mine], yb.at[mine], s2, r2,
+                    device_id={"tm": lax.div(i, n_sp), "space": lax.rem(i, n_sp)}, device_id_type=MESH,
+                ).start()
+
             return carry
 
-        if high > 1:
-            lax.fori_loop(1, high, exchange, 0)
-            wait_bytes(line.at[pl.ds(0, high - 1)], r2)
-        yb[mine] = jnp.sum(line[...], axis=0)
-
-        def gather(i, carry):
-            pltpu.make_async_remote_copy(
-                yb.at[mine], yb.at[mine], s3, r3,
-                device_id=beside(lax.rem(spot + i, side)), device_id_type=MESH,
-            ).start()
-            return carry
-
-        lax.fori_loop(1, side, gather, 0, unroll=side <= 32)
-        wait_bytes(yb.at[pl.ds(0, (owners - 1) * upo)], r3)
-
-    @pl.when(spot >= owners)
+        lax.fori_loop(0, side, gather, 0, unroll=side <= 32)
+        wait_bytes(yb.at[pl.ds(0, (len(owners) - 1) * upo)], r2)
+
+    @pl.when(jnp.logical_not(owner))
     def _():
-        wait_bytes(yb, r3)
+        wait_bytes(yb, r2)
 
     y_out[...] = yb[...]
     for ci in range(len(chunks)):
         wait_bytes(recs[ci].at[pl.ds(0, n_tm - 1)], a_send.at[ci])
 
-    @pl.when(spot < owners)
+    @pl.when(owner)
     def _():
-        wait_bytes(xb.at[pl.ds(0, (owners - 1) * upo)], s1)
-        if high > 1:
-            wait_bytes(line.at[pl.ds(0, high - 1)], s2)
-        wait_bytes(plane.at[pl.ds(0, side - 1)], s3)
-
-    @pl.when(spot >= owners)
+        wait_bytes(xb.at[pl.ds(0, (len(owners) - 1) * upo)], s1)
+        wait_bytes(plane.at[pl.ds(0, side - 1)], s2)
+
+    @pl.when(jnp.logical_not(owner))
     def _():
         wait_bytes(xb, s1)
 
@@ -310,7 +296,11 @@
     diag_k = row_f == lane // modes
     diag_b = row_f == (lane % half) // blocks
     lane2 = lax.broadcasted_iota(jnp.int32, (blocks, lanes), 1)
-    scale = 1.0 / math.sqrt(entries)
+
+    def unit(at):
+        return pairs[at // 2][at % 2 * blocks : (at % 2 + 1) * blocks]
+
+    pairs = [yb[at].astype(F32) for at in range(yb.shape[0])]
 
     def spread_rows(val, mask):
         big = jnp.broadcast_to(val[None], (GROUP, blocks, lanes))
@@ -321,10 +311,9 @@
         top = g * 2 * half
         f0 = g * GROUP
         nf = min(GROUP, freqs - f0)
-        co = [yb[3 * g + c] * scale for c in range(2)]
-        held.append(co)
-        cr, ci = [v.astype(BF).astype(F32) for v in co]
-        gram = yb[3 * g + 2]
+        cr, ci = unit(3 * g), unit(3 * g + 1)
+        held.append((cr, ci))
+        gram = unit(3 * g + 2)
         d_r, d_i = spread_rows(cr, diag_k), spread_rows(ci, diag_k)
         turned = pltpu.roll(gram, half, 1)
         turned = jnp.where(lane2 < half, -turned, turned)
@@ -349,18 +338,16 @@
     e_row = lax.broadcasted_iota(jnp.int32, (lanes, freqs), 0) // modes
     e_col = lax.broadcasted_iota(jnp.int32, (lanes, freqs), 1)
     moves = [jnp.where(e_col == e_row + g * GROUP, 1.0, 0.0).astype(BF) for g in range(groups)]
-    move = jnp.concatenate(moves + moves, axis=0)
+    move = jnp.concatenate(moves, axis=0)
     for c in range(2):
-        his, los = [], []
+        rows = []
         for g in range(groups):
             val = held[g][c]
             if g == groups - 1:
                 val = jnp.where(lane2 < (freqs - g * GROUP) * modes, val, 0.0)
-            hi = val.astype(BF).astype(F32)
-            for part, to in ((hi, his), (val - hi, los)):
-                big = jnp.broadcast_to(part[:, None, :], (blocks, modes, lanes))
-                to.append(jnp.where(pick, big, 0.0).reshape(blocks * modes, lanes).astype(BF))
-        moved = mm(jnp.concatenate(his + los, axis=1), move, ((1,), (0,)))
+            big = jnp.broadcast_to(val[:, None, :], (blocks, modes, lanes))
+            rows.append(jnp.where(pick, big, 0.0).reshape(blocks * modes, lanes).astype(BF))
+        moved = mm(jnp.concatenate(rows, axis=1), move, ((1,), (0,)))
         coef_out[c] = moved.reshape(blocks, modes, freqs)
     for cp in copies:
         cp.wait()
@@ -376,33 +363,31 @@
         blocks = offsets.shape[0]
         groups = -(-freqs // GROUP)
         entries = nvar * pts * n
-        units = 3 * groups
-        low = n_tm
-        side = low * n_sp
-        upo = -(-units // side)
-        owners = -(-units // upo)
+        pairs = -(-3 * groups // 2)
+        side = n_tm * n_sp
+        upo = -(-pairs // side)
+        owners = owner_list(n_tm, n_sp, -(-pairs // upo))
         table_rows = groups * 2 * GROUP * blocks
-        unit = (blocks, GROUP * modes)
+        unit = (2 * blocks, GROUP * modes)
         chunks = tuple((v, min(v + 2, nvar)) for v in range(0, nvar, 2))
         snap = jnp.transpose(snapshots, (1, 0, 2))
         base = jnp.transpose(basis, (0, 1, 3, 2, 4))
         hbm = pl.BlockSpec(memory_space=pltpu.HBM)
         vmem = pl.BlockSpec(memory_space=pltpu.VMEM)
         spec, total = pl.pallas_call(
-            functools.partial(kernel, n_tm, n_sp, low, entries, chunks),
+            functools.partial(kernel, n_tm, n_sp, owners, entries, chunks),
             out_shape=(
                 jax.ShapeDtypeStruct((table_rows, nvar * pts), BF),
-                jax.ShapeDtypeStruct((owners * upo,) + unit, F32),
+                jax.ShapeDtypeStruct((len(owners) * upo,) + unit, BF),
             ),
             in_specs=[hbm] * 5,
             out_specs=(vmem, vmem),
             scratch_shapes=[
                 pltpu.VMEM((table_rows, rows * n_tm), BF),
                 pltpu.VMEM((2, groups * GROUP, nvar, modes, pts), BF),
-                pltpu.VMEM((owners * upo,) + unit, F32),
-                pltpu.VMEM((n_tm // low, upo) + unit, F32),
-                pltpu.VMEM((side, upo) + unit, F32),
-                pltpu.VMEM((owners * upo,) + unit, F32),
+                pltpu.VMEM((len(owners) * upo,) + unit, BF),
+                pltpu.VMEM((side, upo) + unit, BF),
+                pltpu.VMEM((len(owners) * upo,) + unit, BF),
                 pltpu.VMEM(mass_table.shape, F32),
                 pltpu.SMEM(elem_kind.shape, jnp.int32),
                 pltpu.SMEM(offsets.shape, jnp.int32),
@@ -414,7 +399,7 @@
                 pltpu.SemaphoreType.DMA((4,)),
                 pltpu.SemaphoreType.REGULAR((3,)),
             ]
-            + [pltpu.SemaphoreType.DMA] * 6,
+            + [pltpu.SemaphoreType.DMA] * 4,
             compiler_params=pltpu.CompilerParams(
                 collective_id=0, has_side_effects=True, vmem_limit_bytes=48 * 1024 * 1024
             ),

time: 34.3 us -> 33.6 us (0.980)
  Pallas kernels: 33.5 us -> 32.8 us
    pallas_call x1, Pallas kernels: 31.3 us -> 30.7 us  [on_device(): pl.pallas_call(functools.partial(kernel, n_tm, n_sp, owners, entries, chu...]
where the time goes in v2:
time: 33.6 us; the launch traced here: 33.5 us
  Pallas kernels  32.8 us (98%)
  between operations  0.64 us (2%)
    pallas_call x1, Pallas kernels, on_device(): pl.pallas_call(functools.partial(kernel, n_tm, n_sp, owners, entries, chu...  30.7 us
    pallas_call x1, Pallas kernels, on_device(): pl.pallas_call(functools.partial(finish, entries), out_shape=(jax.ShapeDt...  2.14 us

profile of v2, /device:TPU:0, one launch (start us, length us, event | category | flops | bytes accessed | tf_op | source)
XLA Modules:
  0.0 33.5 jit_solution(12664371365000639554)
XLA Ops:
  0.6 30.7 %shard_map.68 = (bf16[640,640]{1,0:T(8,128)(2,1)S(1)}, bf16[8,16,128]{2,1,0:T(8,128)(2,1)S(1)}) custom-call(bf16[5,32,2048]{2,1,0:T(8,128)(2,1)} %bitcast.5, bf16[2,33,5,16,128]{4,3,2,1,0:T(8,128)(2,1)} %bitcast.4, f32[8,64,64]{2,1,0:T(8,128)} %mass_in.1, s32[2]{0:T(128)} %kinds_in.1, s32[8]{0:T(128)} %offs_in.1), custom_call_target="tpu_custom_call" | custom-call | tf_op jit(solution)/shard_map/pallas_call | solution.py:377
  31.3 2.1 %shard_map.69 = (f32[2,8,16,33]{3,2,1,0:T(8,128)}, bf16[2,33,5,16,128]{4,3,2,1,0:T(8,128)(2,1)}) custom-call(bf16[8,16,128]{2,1,0:T(8,128)(2,1)S(1)} %get-tuple-element.6.yb, bf16[640,640]{1,0:T(8,128)(2,1)S(1)} %get-tuple-element.7.sh), custom_call_target="tpu_custom_call" | custom-call | tf_op jit(solution)/shard_map/pallas_call | solution.py:407

commit v3 on v2

--- a/solution.py
+++ b/solution.py
@@ -26,6 +26,21 @@
 
 def mm(a, b, contract):
     return lax.dot_general(a, b, (contract, ((), ())), preferred_element_type=F32)
+
+
+def swap_halves(x, half):
+    lanes = x.shape[1]
+    if 2 * half == lanes:
+        return pltpu.roll(x, half, 1)
+    lane = lax.broadcasted_iota(jnp.int32, x.shape, 1)
+    return jnp.where(lane < half, pltpu.roll(x, lanes - half, 1), pltpu.roll(x, half, 1))
+
+
+def freq_mask(nf, rows, lanes, blocks):
+    row_f = lax.broadcasted_iota(jnp.int32, (nf, rows, lanes), 0)
+    lane = lax.broadcasted_iota(jnp.int32, (nf, rows, lanes), 2)
+    half = nf * blocks
+    return (row_f == lane % half // blocks) & (lane < 2 * half)
 
 
 def kernel(
@@ -49,13 +64,13 @@
     inward = jnp.where(lev < LEVELS // 2, 1, -1)
     freqs = basis.shape[1]
     rows, pts = recs[0].shape[2:]
-    groups = sh.shape[0] // (2 * GROUP * 8)
+    groups = -(-freqs // GROUP)
+    counts = [min(GROUP, freqs - g * GROUP) for g in range(groups)]
     record = n_tm * rows
     blocks = offs.shape[0]
     modes = basis.shape[3]
     upo = plane.shape[1]
-    half = GROUP * blocks
-    lanes = GROUP * modes
+    lanes = 2 * GROUP * blocks
 
     barrier = pltpu.get_barrier_semaphore()
 
@@ -84,7 +99,7 @@
         pltpu.make_async_copy(offs_in, offs, l_sem.at[0]),
         pltpu.make_async_copy(kinds_in, kinds, l_sem.at[1]),
         pltpu.make_async_copy(mass_in, mass, l_sem.at[2]),
-        pltpu.make_async_copy(basis, ub.at[:, pl.ds(0, freqs)], l_sem.at[3]),
+        pltpu.make_async_copy(basis, ub, l_sem.at[3]),
     ]
     for cp in loads:
         cp.start()
@@ -156,12 +171,14 @@
     c1, s1v = jnp.cos(theta), jnp.sin(theta)
     win = jnp.where(inside, (0.5 - 0.5 * c1) * (1.0 / math.sqrt(0.375 * NT)), 0.0)
     cc, ss = win, jnp.zeros_like(win)
-    for f in range(0, groups * GROUP, 2):
-        c_next, s_next = cc * c1 - ss * s1v, ss * c1 + cc * s1v
-        at = (f // GROUP) * 2 * half + (f % GROUP) * blocks
-        table[at : at + 2 * blocks] = jnp.concatenate([cc, c_next], axis=0).astype(BF)
-        table[at + half : at + half + 2 * blocks] = jnp.concatenate([-ss, -s_next], axis=0).astype(BF)
-        cc, ss = c_next * c1 - s_next * s1v, s_next * c1 + c_next * s1v
+    for g, nf in enumerate(counts):
+        parts = []
+        for _ in range(nf):
+            parts.append((cc, -ss))
+            cc, ss = cc * c1 - ss * s1v, ss * c1 + cc * s1v
+        table[g * lanes : g * lanes + 2 * nf * blocks] = jnp.concatenate(
+            [p[c] for c in range(2) for p in parts], axis=0
+        ).astype(BF)
 
     loads[1].wait()
     loads[2].wait()
@@ -181,18 +198,17 @@
     m_stack = jnp.concatenate([m_hi, m_hi, m_lo], axis=0)
 
     loads[3].wait()
-    ub[:, freqs:] = jnp.zeros((2, groups * GROUP - freqs) + ub.shape[2:], BF)
-
-    row_f = lax.broadcasted_iota(jnp.int32, (GROUP, blocks, lanes), 0)
-    lane = lax.broadcasted_iota(jnp.int32, (GROUP, blocks, lanes), 2)
-    diag_k = row_f == lane // modes
-    diag_b = row_f == (lane % half) // blocks
-    lane2 = lax.broadcasted_iota(jnp.int32, (blocks, lanes), 1)
-
-    def fold(full, mask):
-        return jnp.sum(jnp.where(mask, full.reshape(GROUP, blocks, lanes), 0.0), axis=0)
-
-    total = [None] * (3 * groups)
+    def fold(full, nf, rows):
+        mask = freq_mask(nf, rows, lanes, blocks)
+        real, imag = [
+            jnp.sum(jnp.where(mask, part.reshape(nf, rows, lanes), 0.0), axis=0)
+            for part in (full[: nf * rows], full[nf * rows :])
+        ]
+        imag = swap_halves(imag, nf * blocks)
+        lane = lax.broadcasted_iota(jnp.int32, (rows, lanes), 1)
+        return real + jnp.where(lane < nf * blocks, imag, -imag)
+
+    coefs, grams = [None] * groups, [None] * groups
     for ci, (v0, v1) in enumerate(chunks):
         rec = recs[ci]
         pltpu.make_async_copy(rec, rec, a_recv.at[ci]).wait()
@@ -208,31 +224,28 @@
             lhs = jnp.concatenate([s_hi[:, cut], s_lo[:, cut], s_hi[:, cut]], axis=1)
             wts.append(mm(lhs, m_stack, ((1,), (0,))).astype(BF))
         wt = jnp.concatenate(wts, axis=1)
-        for g in range(groups):
-            top = g * 2 * half
+        for g, nf in enumerate(counts):
+            cut = slice(g * lanes, g * lanes + 2 * nf * blocks)
             f0 = g * GROUP
             u = [
                 jnp.concatenate(
-                    [ub[c, f0 : f0 + GROUP, v].reshape(lanes, pts) for v in range(v0, v1)], axis=1
+                    [ub[c, f0 : f0 + nf, v].reshape(nf * modes, pts) for v in range(v0, v1)], axis=1
                 )
                 for c in range(2)
             ]
-            lhs = jnp.concatenate(u + [s_hi[top : top + 2 * half]], axis=0)
-            full = mm(wt[top : top + 2 * half], lhs, ((1,), (1,)))
-            rr = fold(full[:half, :lanes], diag_k)
-            ri = fold(full[:half, lanes : 2 * lanes], diag_k)
-            ir = fold(full[half:, :lanes], diag_k)
-            ii = fold(full[half:, lanes : 2 * lanes], diag_k)
-            p_r = fold(full[:half, 2 * lanes :], diag_b)
-            p_i = pltpu.roll(fold(full[half:, 2 * lanes :], diag_b), half, 1)
-            new = [(rr + ii) * scale, (ir - ri) * scale, jnp.where(lane2 < half, p_r + p_i, p_i - p_r)]
-            for j in range(3):
-                at = 3 * g + j
-                total[at] = new[j] if ci == 0 else total[at] + new[j]
-    empty = jnp.zeros((blocks, lanes), F32)
-    total += [empty] * (2 * xb.shape[0] - len(total))
-    for at in range(xb.shape[0]):
-        xb[at] = jnp.concatenate(total[2 * at : 2 * at + 2], axis=0).astype(BF)
+            w = wt[cut]
+            if w.shape[0] < lanes:
+                w = jnp.concatenate([w, jnp.zeros((lanes - w.shape[0], w.shape[1]), BF)], axis=0)
+            full = mm(jnp.concatenate(u + [s_hi[cut]], axis=0), w, ((1,), (1,)))
+            coef = fold(full[: 2 * nf * modes], nf, modes) * scale
+            gram = fold(full[2 * nf * modes :], nf, blocks)
+            coefs[g] = coef if ci == 0 else coefs[g] + coef
+            grams[g] = gram if ci == 0 else grams[g] + gram
+    grams += [jnp.zeros_like(grams[0])] * (groups % 2)
+    for at, tile in enumerate(
+        coefs + [jnp.concatenate(grams[i : i + 2], axis=0) for i in range(0, groups, 2)]
+    ):
+        xb[at] = tile.astype(BF)
 
     pl.semaphore_wait(known.at[2], n_sp - 1)
     for o, (o_tm, o_sp) in enumerate(owners):
@@ -288,66 +301,57 @@
 def finish(entries, yb, sh, coef_out, new_out, ob, o_sem):
     freqs, nvar, modes, pts = new_out.shape[1:]
     blocks = coef_out.shape[1]
-    half = GROUP * blocks
-    lanes = GROUP * modes
+    lanes = yb.shape[2]
     groups = -(-freqs // GROUP)
-    row_f = lax.broadcasted_iota(jnp.int32, (GROUP, blocks, lanes), 0)
-    lane = lax.broadcasted_iota(jnp.int32, (GROUP, blocks, lanes), 2)
-    diag_k = row_f == lane // modes
-    diag_b = row_f == (lane % half) // blocks
-    lane2 = lax.broadcasted_iota(jnp.int32, (blocks, lanes), 1)
-
-    def unit(at):
-        return pairs[at // 2][at % 2 * blocks : (at % 2 + 1) * blocks]
-
-    pairs = [yb[at].astype(F32) for at in range(yb.shape[0])]
-
-    def spread_rows(val, mask):
-        big = jnp.broadcast_to(val[None], (GROUP, blocks, lanes))
-        return jnp.where(mask, big, 0.0).reshape(half, lanes)
-
-    copies, held = [], []
+    lane = lax.broadcasted_iota(jnp.int32, (modes, lanes), 1)
+    lane_b = lane[:blocks]
+
+    copies, tiles = [], []
     for g in range(groups):
-        top = g * 2 * half
         f0 = g * GROUP
         nf = min(GROUP, freqs - f0)
-        cr, ci = unit(3 * g), unit(3 * g + 1)
-        held.append((cr, ci))
-        gram = unit(3 * g + 2)
-        d_r, d_i = spread_rows(cr, diag_k), spread_rows(ci, diag_k)
-        turned = pltpu.roll(gram, half, 1)
-        turned = jnp.where(lane2 < half, -turned, turned)
-        quad = jnp.concatenate([spread_rows(gram, diag_b), spread_rows(turned, diag_b)], axis=0)
-        vec = jnp.concatenate([d_r, d_i], axis=0)
-        energy = jnp.sum(vec * mm(quad.astype(BF), vec.astype(BF), ((1,), (0,))), axis=0, keepdims=True)
+        half = nf * blocks
+
+        def spread(val):
+            rows = val.shape[0]
+            big = jnp.broadcast_to(val[None], (nf, rows, lanes))
+            return jnp.where(freq_mask(nf, rows, lanes, blocks), big, 0.0).reshape(nf * rows, lanes)
+
+        coef = yb[g].astype(F32)
+        gram = yb[groups + g // 2].astype(F32)[g % 2 * blocks : (g % 2 + 1) * blocks]
+        tiles.append(coef)
+        vec = spread(jnp.where(lane < half, coef, -coef))
+        turned = swap_halves(gram, half)
+        quad = jnp.concatenate([spread(gram), spread(jnp.where(lane_b < half, -turned, turned))], axis=0)
+        rows = [vec[:, : 2 * half].astype(BF), spread(swap_halves(coef, half))[:, : 2 * half].astype(BF)]
+        energy = jnp.sum(vec * mm(rows[0], quad.astype(BF), ((1,), (0,))), axis=1, keepdims=True)
         factor = 1.0 / jnp.sqrt(energy / entries + 1e-06)
-        fac = jnp.transpose(jnp.broadcast_to(factor, (pts, lanes)))
-        s_g = sh[top : top + 2 * half]
+        s_g = sh[g * lanes : g * lanes + 2 * half]
         for c in range(2):
-            d = jnp.concatenate([d_r, -d_i] if c == 0 else [d_i, d_r], axis=0)
-            field = mm(jnp.transpose(d).astype(BF), s_g, ((1,), (0,)))
+            field = mm(rows[c], s_g, ((1,), (0,)))
             for v in range(nvar):
-                val = (field[:, v * pts : (v + 1) * pts] * fac).astype(BF).reshape(GROUP, modes, pts)
-                ob[c, f0 : f0 + nf, v] = val[:nf]
+                val = (field[:, v * pts : (v + 1) * pts] * factor).astype(BF)
+                ob[c, f0 : f0 + nf, v] = val.reshape(nf, modes, pts)
         cp = pltpu.make_async_copy(ob.at[:, pl.ds(f0, nf)], new_out.at[:, pl.ds(f0, nf)], o_sem.at[g])
         cp.start()
         copies.append(cp)
 
-    mode_row = lax.broadcasted_iota(jnp.int32, (blocks, modes, lanes), 1)
-    pick = mode_row == lax.broadcasted_iota(jnp.int32, (blocks, modes, lanes), 2) % modes
-    e_row = lax.broadcasted_iota(jnp.int32, (lanes, freqs), 0) // modes
-    e_col = lax.broadcasted_iota(jnp.int32, (lanes, freqs), 1)
-    moves = [jnp.where(e_col == e_row + g * GROUP, 1.0, 0.0).astype(BF) for g in range(groups)]
-    move = jnp.concatenate(moves, axis=0)
+    row_b = lax.broadcasted_iota(jnp.int32, (blocks, modes, lanes), 0)
+    pick = row_b == lax.broadcasted_iota(jnp.int32, (blocks, modes, lanes), 2) % blocks
+    picked = [
+        jnp.where(pick, jnp.broadcast_to(t[None], pick.shape), 0.0).reshape(blocks * modes, lanes)
+        for t in tiles
+    ]
+    lhs = jnp.concatenate(picked, axis=1).astype(BF)
+    row = lax.broadcasted_iota(jnp.int32, (lanes, freqs), 0)
+    col = lax.broadcasted_iota(jnp.int32, (lanes, freqs), 1)
     for c in range(2):
-        rows = []
+        moves = []
         for g in range(groups):
-            val = held[g][c]
-            if g == groups - 1:
-                val = jnp.where(lane2 < (freqs - g * GROUP) * modes, val, 0.0)
-            big = jnp.broadcast_to(val[:, None, :], (blocks, modes, lanes))
-            rows.append(jnp.where(pick, big, 0.0).reshape(blocks * modes, lanes).astype(BF))
-        moved = mm(jnp.concatenate(rows, axis=1), move, ((1,), (0,)))
+            half = min(GROUP, freqs - g * GROUP) * blocks
+            hit = (row // half == c) & (col == row % half // blocks + g * GROUP)
+            moves.append(jnp.where(hit, 1.0, 0.0).astype(BF))
+        moved = mm(lhs, jnp.concatenate(moves, axis=0), ((1,), (0,)))
         coef_out[c] = moved.reshape(blocks, modes, freqs)
     for cp in copies:
         cp.wait()
@@ -363,12 +367,12 @@
         blocks = offsets.shape[0]
         groups = -(-freqs // GROUP)
         entries = nvar * pts * n
-        pairs = -(-3 * groups // 2)
+        pairs = groups + -(-groups // 2)
         side = n_tm * n_sp
         upo = -(-pairs // side)
         owners = owner_list(n_tm, n_sp, -(-pairs // upo))
-        table_rows = groups * 2 * GROUP * blocks
-        unit = (2 * blocks, GROUP * modes)
+        table_rows = 2 * freqs * blocks
+        unit = (2 * blocks, 2 * GROUP * blocks)
         chunks = tuple((v, min(v + 2, nvar)) for v in range(0, nvar, 2))
         snap = jnp.transpose(snapshots, (1, 0, 2))
         base = jnp.transpose(basis, (0, 1, 3, 2, 4))
@@ -384,7 +388,7 @@
             out_specs=(vmem, vmem),
             scratch_shapes=[
                 pltpu.VMEM((table_rows, rows * n_tm), BF),
-                pltpu.VMEM((2, groups * GROUP, nvar, modes, pts), BF),
+                pltpu.VMEM((2, freqs, nvar, modes, pts), BF),
                 pltpu.VMEM((len(owners) * upo,) + unit, BF),
                 pltpu.VMEM((side, upo) + unit, BF),
                 pltpu.VMEM((len(owners) * upo,) + unit, BF),

time: 33.6 us -> 33.6 us (level)
  no operation moved by 1% of the time
where the time goes in v3:
time: 33.6 us; the launch traced here: 33.4 us
  Pallas kernels  32.8 us (98%)
  between operations  0.64 us (2%)
    pallas_call x1, Pallas kernels, on_device(): pl.pallas_call(functools.partial(kernel, n_tm, n_sp, owners, entries, chu...  30.7 us
    pallas_call x1, Pallas kernels, on_device(): pl.pallas_call(functools.partial(finish, entries), out_shape=(jax.ShapeDt...  2.11 us

profile of v3, /device:TPU:0, one launch (start us, length us, event | category | flops | bytes accessed | tf_op | source)
XLA Modules:
  0.0 33.4 jit_solution(14518220729103267281)
XLA Ops:
  0.6 30.7 %shard_map.68 = (bf16[528,640]{1,0:T(8,128)(2,1)S(1)}, bf16[8,16,128]{2,1,0:T(8,128)(2,1)S(1)}) custom-call(bf16[5,32,2048]{2,1,0:T(8,128)(2,1)} %bitcast.5, bf16[2,33,5,16,128]{4,3,2,1,0:T(8,128)(2,1)} %bitcast.4, f32[8,64,64]{2,1,0:T(8,128)} %mass_in.1, s32[2]{0:T(128)} %kinds_in.1, s32[8]{0:T(128)} %offs_in.1), custom_call_target="tpu_custom_call" | custom-call | tf_op jit(solution)/shard_map/pallas_call | solution.py:381
  31.3 2.1 %shard_map.69 = (f32[2,8,16,33]{3,2,1,0:T(8,128)}, bf16[2,33,5,16,128]{4,3,2,1,0:T(8,128)(2,1)}) custom-call(bf16[8,16,128]{2,1,0:T(8,128)(2,1)S(1)} %get-tuple-element.6.yb, bf16[528,640]{1,0:T(8,128)(2,1)S(1)} %get-tuple-element.7.sh), custom_call_target="tpu_custom_call" | custom-call | tf_op jit(solution)/shard_map/pallas_call | solution.py:411

commit v4 on v3

--- a/solution.py
+++ b/solution.py
@@ -298,7 +298,7 @@
         wait_bytes(xb, s1)
 
 
-def finish(entries, yb, sh, coef_out, new_out, ob, o_sem):
+def finish(entries, yb, sh, coef_hbm, new_out, ob, coef_out, o_sem):
     freqs, nvar, modes, pts = new_out.shape[1:]
     blocks = coef_out.shape[1]
     lanes = yb.shape[2]
@@ -306,36 +306,7 @@
     lane = lax.broadcasted_iota(jnp.int32, (modes, lanes), 1)
     lane_b = lane[:blocks]
 
-    copies, tiles = [], []
-    for g in range(groups):
-        f0 = g * GROUP
-        nf = min(GROUP, freqs - f0)
-        half = nf * blocks
-
-        def spread(val):
-            rows = val.shape[0]
-            big = jnp.broadcast_to(val[None], (nf, rows, lanes))
-            return jnp.where(freq_mask(nf, rows, lanes, blocks), big, 0.0).reshape(nf * rows, lanes)
-
-        coef = yb[g].astype(F32)
-        gram = yb[groups + g // 2].astype(F32)[g % 2 * blocks : (g % 2 + 1) * blocks]
-        tiles.append(coef)
-        vec = spread(jnp.where(lane < half, coef, -coef))
-        turned = swap_halves(gram, half)
-        quad = jnp.concatenate([spread(gram), spread(jnp.where(lane_b < half, -turned, turned))], axis=0)
-        rows = [vec[:, : 2 * half].astype(BF), spread(swap_halves(coef, half))[:, : 2 * half].astype(BF)]
-        energy = jnp.sum(vec * mm(rows[0], quad.astype(BF), ((1,), (0,))), axis=1, keepdims=True)
-        factor = 1.0 / jnp.sqrt(energy / entries + 1e-06)
-        s_g = sh[g * lanes : g * lanes + 2 * half]
-        for c in range(2):
-            field = mm(rows[c], s_g, ((1,), (0,)))
-            for v in range(nvar):
-                val = (field[:, v * pts : (v + 1) * pts] * factor).astype(BF)
-                ob[c, f0 : f0 + nf, v] = val.reshape(nf, modes, pts)
-        cp = pltpu.make_async_copy(ob.at[:, pl.ds(f0, nf)], new_out.at[:, pl.ds(f0, nf)], o_sem.at[g])
-        cp.start()
-        copies.append(cp)
-
+    copies, tiles = [], [yb[g].astype(F32) for g in range(groups)]
     row_b = lax.broadcasted_iota(jnp.int32, (blocks, modes, lanes), 0)
     pick = row_b == lax.broadcasted_iota(jnp.int32, (blocks, modes, lanes), 2) % blocks
     picked = [
@@ -353,6 +324,38 @@
             moves.append(jnp.where(hit, 1.0, 0.0).astype(BF))
         moved = mm(lhs, jnp.concatenate(moves, axis=0), ((1,), (0,)))
         coef_out[c] = moved.reshape(blocks, modes, freqs)
+    cp = pltpu.make_async_copy(coef_out, coef_hbm, o_sem.at[groups])
+    cp.start()
+    copies.append(cp)
+
+    for g in range(groups):
+        f0 = g * GROUP
+        nf = min(GROUP, freqs - f0)
+        half = nf * blocks
+
+        def spread(val):
+            rows = val.shape[0]
+            big = jnp.broadcast_to(val[None], (nf, rows, lanes))
+            return jnp.where(freq_mask(nf, rows, lanes, blocks), big, 0.0).reshape(nf * rows, lanes)
+
+        coef = tiles[g]
+        gram = yb[groups + g // 2].astype(F32)[g % 2 * blocks : (g % 2 + 1) * blocks]
+        vec = spread(jnp.where(lane < half, coef, -coef))
+        turned = swap_halves(gram, half)
+        quad = jnp.concatenate([spread(gram), spread(jnp.where(lane_b < half, -turned, turned))], axis=0)
+        rows = [vec[:, : 2 * half].astype(BF), spread(swap_halves(coef, half))[:, : 2 * half].astype(BF)]
+        energy = jnp.sum(vec * mm(rows[0], quad.astype(BF), ((1,), (0,))), axis=1, keepdims=True)
+        factor = 1.0 / jnp.sqrt(energy / entries + 1e-06)
+        s_g = sh[g * lanes : g * lanes + 2 * half]
+        for c in range(2):
+            field = mm(rows[c], s_g, ((1,), (0,)))
+            for v in range(nvar):
+                val = (field[:, v * pts : (v + 1) * pts] * factor).astype(BF)
+                ob[c, f0 : f0 + nf, v] = val.reshape(nf, modes, pts)
+        cp = pltpu.make_async_copy(ob.at[:, pl.ds(f0, nf)], new_out.at[:, pl.ds(f0, nf)], o_sem.at[g])
+        cp.start()
+        copies.append(cp)
+
     for cp in copies:
         cp.wait()
 
@@ -415,8 +418,12 @@
                 jax.ShapeDtypeStruct(base.shape, BF),
             ),
             in_specs=[vmem, vmem],
-            out_specs=(vmem, hbm),
-            scratch_shapes=[pltpu.VMEM(base.shape, BF), pltpu.SemaphoreType.DMA((groups,))],
+            out_specs=(hbm, hbm),
+            scratch_shapes=[
+                pltpu.VMEM(base.shape, BF),
+                pltpu.VMEM((2, blocks, modes, freqs), F32),
+                pltpu.SemaphoreType.DMA((groups + 1,)),
+            ],
             compiler_params=pltpu.CompilerParams(vmem_limit_bytes=32 * 1024 * 1024),
         )(total, spec)
         return jnp.transpose(coef, (0, 3, 1, 2)), jnp.transpose(new, (0, 1, 3, 2, 4))

time: 33.6 us -> 32.9 us (0.979)
  Pallas kernels: 32.8 us -> 32.2 us
    pallas_call x1, Pallas kernels: 2.11 us -> 1.48 us  [on_device(): pl.pallas_call(functools.partial(finish, entries), out_shape=(jax.ShapeDt...]
where the time goes in v4:
time: 32.9 us; the launch traced here: 32.8 us
  Pallas kernels  32.2 us (98%)
  between operations  0.64 us (2%)
    pallas_call x1, Pallas kernels, on_device(): pl.pallas_call(functools.partial(kernel, n_tm, n_sp, owners, entries, chu...  30.7 us
    pallas_call x1, Pallas kernels, on_device(): pl.pallas_call(functools.partial(finish, entries), out_shape=(jax.ShapeDt...  1.48 us

profile of v4, /device:TPU:0, one launch (start us, length us, event | category | flops | bytes accessed | tf_op | source)
XLA Modules:
  0.0 32.8 jit_solution(15051968903519885400)
XLA Ops:
  0.6 30.7 %shard_map.68 = (bf16[528,640]{1,0:T(8,128)(2,1)S(1)}, bf16[8,16,128]{2,1,0:T(8,128)(2,1)S(1)}) custom-call(bf16[5,32,2048]{2,1,0:T(8,128)(2,1)} %bitcast.5, bf16[2,33,5,16,128]{4,3,2,1,0:T(8,128)(2,1)} %bitcast.4, f32[8,64,64]{2,1,0:T(8,128)} %mass_in.1, s32[2]{0:T(128)} %kinds_in.1, s32[8]{0:T(128)} %offs_in.1), custom_call_target="tpu_custom_call" | custom-call | tf_op jit(solution)/shard_map/pallas_call | solution.py:384
  31.3 1.5 %shard_map.69 = (f32[2,8,16,33]{3,2,1,0:T(8,128)}, bf16[2,33,5,16,128]{4,3,2,1,0:T(8,128)(2,1)}) custom-call(bf16[8,16,128]{2,1,0:T(8,128)(2,1)S(1)} %get-tuple-element.6.yb, bf16[528,640]{1,0:T(8,128)(2,1)S(1)} %get-tuple-element.7.sh), custom_call_target="tpu_custom_call" | custom-call | tf_op jit(solution)/shard_map/pallas_call | solution.py:414

commit v5 on v4

--- a/solution.py
+++ b/solution.py
@@ -18,10 +18,9 @@
 
 def owner_list(n_tm, n_sp, count):
     quart = n_tm // LEVELS
-    first = [(quart, 0), (2 * quart, 0), (quart + 2, 0), (quart, 1)]
-    spots = [(t + c, s) for t, s in first for c in range(2)]
-    spots += [(t, s) for s in range(n_sp) for t in range(n_tm) if (t, s) not in spots]
-    return tuple(p for p in spots if p[0] < n_tm and p[1] < n_sp)[:count]
+    spots = [(t % n_tm, s) for t in range(quart, quart + n_tm, 2) for s in range(n_sp)]
+    spots = [(t + c, s) for t, s in spots for c in range(2)]
+    return tuple(spots[:count])
 
 
 def mm(a, b, contract):
@@ -214,7 +213,8 @@
         pltpu.make_async_copy(rec, rec, a_recv.at[ci]).wait()
         count = v1 - v0
         x = jnp.concatenate([rec[:, v].reshape(record, pts) for v in range(count)], axis=1)
-        spec = mm(table[...], x, ((1,), (0,)))
+        cuts = [0, table.shape[0]] if count > 1 else [0, lanes * (groups // 2), table.shape[0]]
+        spec = jnp.concatenate([mm(table[i:j], x, ((1,), (0,))) for i, j in zip(cuts, cuts[1:])], axis=0)
         s_hi = spec.astype(BF)
         s_lo = (spec - s_hi.astype(F32)).astype(BF)
         sh[:, v0 * pts : v1 * pts] = s_hi
@@ -222,7 +222,11 @@
         for v in range(count):
             cut = slice(v * pts, (v + 1) * pts)
             lhs = jnp.concatenate([s_hi[:, cut], s_lo[:, cut], s_hi[:, cut]], axis=1)
-            wts.append(mm(lhs, m_stack, ((1,), (0,))).astype(BF))
+            wts.append(
+                jnp.concatenate(
+                    [mm(lhs[i:j], m_stack, ((1,), (0,))).astype(BF) for i, j in zip(cuts, cuts[1:])], axis=0
+                )
+            )
         wt = jnp.concatenate(wts, axis=1)
         for g, nf in enumerate(counts):
             cut = slice(g * lanes, g * lanes + 2 * nf * blocks)
@@ -346,11 +350,11 @@
         rows = [vec[:, : 2 * half].astype(BF), spread(swap_halves(coef, half))[:, : 2 * half].astype(BF)]
         energy = jnp.sum(vec * mm(rows[0], quad.astype(BF), ((1,), (0,))), axis=1, keepdims=True)
         factor = 1.0 / jnp.sqrt(energy / entries + 1e-06)
-        s_g = sh[g * lanes : g * lanes + 2 * half]
-        for c in range(2):
-            field = mm(rows[c], s_g, ((1,), (0,)))
-            for v in range(nvar):
-                val = (field[:, v * pts : (v + 1) * pts] * factor).astype(BF)
+        both = jnp.concatenate(rows, axis=0)
+        whole = mm(both, sh[g * lanes : g * lanes + 2 * half], ((1,), (0,)))
+        for v in range(nvar):
+            for c in range(2):
+                val = (whole[c * nf * modes : (c + 1) * nf * modes, v * pts : (v + 1) * pts] * factor).astype(BF)
                 ob[c, f0 : f0 + nf, v] = val.reshape(nf, modes, pts)
         cp = pltpu.make_async_copy(ob.at[:, pl.ds(f0, nf)], new_out.at[:, pl.ds(f0, nf)], o_sem.at[g])
         cp.start()

time: 32.9 us -> 32.1 us (0.976)
  Pallas kernels: 32.2 us -> 31.3 us
    pallas_call x1, Pallas kernels: 30.7 us -> 29.9 us  [on_device(): pl.pallas_call(functools.partial(kernel, n_tm, n_sp, owners, entries, chu...]
where the time goes in v5:
time: 32.1 us; the launch traced here: 32 us
  Pallas kernels  31.3 us (98%)
  between operations  0.64 us (2%)
    pallas_call x1, Pallas kernels, on_device(): pl.pallas_call(functools.partial(kernel, n_tm, n_sp, owners, entries, chu...  29.9 us
    pallas_call x1, Pallas kernels, on_device(): pl.pallas_call(functools.partial(finish, entries), out_shape=(jax.ShapeDt...  1.48 us

profile of v5, /device:TPU:0, one launch (start us, length us, event | category | flops | bytes accessed | tf_op | source)
XLA Modules:
  0.0 32.0 jit_solution(15265905485035968045)
XLA Ops:
  0.6 29.9 %shard_map.68 = (bf16[528,640]{1,0:T(8,128)(2,1)S(1)}, bf16[8,16,128]{2,1,0:T(8,128)(2,1)S(1)}) custom-call(bf16[5,32,2048]{2,1,0:T(8,128)(2,1)} %bitcast.5, bf16[2,33,5,16,128]{4,3,2,1,0:T(8,128)(2,1)} %bitcast.4, f32[8,64,64]{2,1,0:T(8,128)} %mass_in.1, s32[2]{0:T(128)} %kinds_in.1, s32[8]{0:T(128)} %offs_in.1), custom_call_target="tpu_custom_call" | custom-call | tf_op jit(solution)/shard_map/pallas_call | solution.py:388
  30.5 1.5 %shard_map.69 = (f32[2,8,16,33]{3,2,1,0:T(8,128)}, bf16[2,33,5,16,128]{4,3,2,1,0:T(8,128)(2,1)}) custom-call(bf16[8,16,128]{2,1,0:T(8,128)(2,1)S(1)} %get-tuple-element.6.yb, bf16[528,640]{1,0:T(8,128)(2,1)S(1)} %get-tuple-element.7.sh), custom_call_target="tpu_custom_call" | custom-call | tf_op jit(solution)/shard_map/pallas_call | solution.py:418

commit v6 on v5

--- a/solution.py
+++ b/solution.py
@@ -16,11 +16,24 @@
 F32 = jnp.float32
 
 
-def owner_list(n_tm, n_sp, count):
+def owner_list(n_tm, n_sp, units):
     quart = n_tm // LEVELS
-    spots = [(t % n_tm, s) for t in range(quart, quart + n_tm, 2) for s in range(n_sp)]
-    spots = [(t + c, s) for t, s in spots for c in range(2)]
-    return tuple(spots[:count])
+    chips = [(quart, 0), (quart + 2, 0), (quart, n_sp - 1)]
+    spots = [(t + c, s) for t, s in chips for c in range(2)]
+    each, extra = divmod(units, len(spots))
+    sizes = [each + (i < extra) for i in range(len(spots))]
+    return tuple((t, s, sum(sizes[:i]), sizes[i]) for i, (t, s) in enumerate(spots))
+
+
+def tail_width(freqs, blocks, modes):
+    width = 2 * (freqs % GROUP) * blocks
+    return width if 0 < width * (1 + modes // blocks) <= 2 * GROUP * blocks else 0
+
+
+def unit_count(freqs, blocks, modes):
+    groups = -(-freqs // GROUP)
+    per = 1 + modes // blocks
+    return groups * per - (per - 1 if tail_width(freqs, blocks, modes) else 0)
 
 
 def mm(a, b, contract):
@@ -54,9 +67,7 @@
     side = n_tm * n_sp
     scale = 1.0 / math.sqrt(entries)
     here = sp * n_tm + tm
-    is_own = [(tm == o_tm) & (sp == o_sp) for o_tm, o_sp in owners]
-    owner = functools.reduce(jnp.logical_or, is_own)
-    spot = sum(jnp.where(m, o, 0) for o, m in enumerate(is_own))
+    is_own = [(tm == t) & (sp == s) for t, s, _, _ in owners]
     quart = n_tm // LEVELS
     lev, place = lax.div(tm, quart), lax.rem(tm, quart)
     edge = (lev == 0) | (lev == LEVELS - 1)
@@ -68,7 +79,6 @@
     record = n_tm * rows
     blocks = offs.shape[0]
     modes = basis.shape[3]
-    upo = plane.shape[1]
     lanes = 2 * GROUP * blocks
 
     barrier = pltpu.get_barrier_semaphore()
@@ -85,7 +95,7 @@
             signal(barrier, to, sp)
             return carry
 
-        @pl.when((lev + dl >= 0) & (lev + dl < LEVELS))
+        @pl.when((lev + dl >= 0) & (lev + dl < LEVELS) & ((dl != -1) | (lev <= LEVELS // 2)))
         def _():
             lax.fori_loop(1 if dl == 0 else 0, quart, greet, 0, unroll=side <= 32)
 
@@ -102,11 +112,11 @@
     ]
     for cp in loads:
         cp.start()
-    near = jnp.where(edge, 2, 3)
+    near = jnp.where((lev == 0) | (lev >= LEVELS // 2), 2, 3)
     pl.semaphore_wait(barrier, near * quart - 1 + n_sp - 1)
 
-    def relay(stage):
-        for dl in (1, -1):
+    def relay(stage, ways=(1, -1)):
+        for dl in ways:
             seen = lev - dl * (stage - 1)
 
             @pl.when((seen >= 0) & (seen < LEVELS) & (lev + dl >= 0) & (lev + dl < LEVELS))
@@ -134,16 +144,26 @@
 
         lax.fori_loop(first, quart, send, 0, unroll=side <= 32)
 
-    relay(2)
+    turn = lev == LEVELS // 2
+    pl.when(jnp.logical_not(turn))(lambda: relay(2))
+    pl.when(lev > LEVELS // 2)(lambda: signal(known.at[3], tm - quart, sp))
     for ci, (v0, v1) in enumerate(chunks):
         mine = snap.at[pl.ds(v0, v1 - v0), :, pl.ds(pl.multiple_of(tm * pts, pts), pts)]
         if ci == 0:
             send_level(ci, lev + inward)
-            pl.when(jnp.logical_not(edge))(lambda: send_level(ci, lev - inward))
+            pl.when(jnp.logical_not(edge | turn))(lambda: send_level(ci, lev - inward))
             send_level(ci, lev, 1)
             learn(2)
-            relay(3)
+            pl.when(jnp.logical_not(turn))(lambda: relay(3))
             send_level(ci, lev + 2 * inward)
+
+            @pl.when(turn)
+            def _():
+                pl.semaphore_wait(known.at[3], 1)
+                relay(2)
+                relay(3)
+                send_level(ci, lev - inward)
+
             learn(3)
             pl.when(edge)(lambda: send_level(ci, lev + 3 * inward))
 
@@ -245,59 +265,79 @@
             gram = fold(full[2 * nf * modes :], nf, blocks)
             coefs[g] = coef if ci == 0 else coefs[g] + coef
             grams[g] = gram if ci == 0 else grams[g] + gram
-    grams += [jnp.zeros_like(grams[0])] * (groups % 2)
-    for at, tile in enumerate(
-        coefs + [jnp.concatenate(grams[i : i + 2], axis=0) for i in range(0, groups, 2)]
-    ):
+    width = tail_width(freqs, blocks, modes)
+    per = modes // blocks
+    tiles = [t for c in coefs for t in (c[i * blocks : (i + 1) * blocks] for i in range(per))]
+    if width:
+        lane = lax.broadcasted_iota(jnp.int32, (blocks, lanes), 1)
+        tail = grams.pop()
+        for i, t in enumerate(tiles[-per:]):
+            tail = jnp.where(lane < (i + 1) * width, tail, pltpu.roll(t, (i + 1) * width, 1))
+        tiles = tiles[:-per] + grams + [tail]
+    else:
+        tiles = tiles + grams
+    for at, tile in enumerate(tiles):
         xb[at] = tile.astype(BF)
 
     pl.semaphore_wait(known.at[2], n_sp - 1)
-    for o, (o_tm, o_sp) in enumerate(owners):
-
-        @pl.when((tm != o_tm) | (sp != o_sp))
+    units = xb.shape[0]
+    for t, s, first, size in owners:
+
+        @pl.when((tm != t) | (sp != s))
         def _():
             pltpu.make_async_remote_copy(
-                xb.at[pl.ds(o * upo, upo)], plane.at[here], s1, r1,
-                device_id={"tm": o_tm, "space": o_sp}, device_id_type=MESH,
+                xb.at[pl.ds(first, size)], plane.at[here, pl.ds(0, size)], s1, r1,
+                device_id={"tm": t, "space": s}, device_id_type=MESH,
             ).start()
 
     def wait_bytes(ref, sem):
         pltpu.make_async_copy(ref, ref, sem).wait()
 
-    @pl.when(owner)
-    def _():
-        mine = pl.ds(spot * upo, upo)
-        plane[here] = xb[mine]
-        wait_bytes(plane.at[pl.ds(0, side - 1)], r1)
-        yb[mine] = jnp.sum(plane[...].astype(F32), axis=0).astype(BF)
-
-        def gather(i, carry):
-            @pl.when(i != tm * n_sp + sp)
-            def _():
-                pltpu.make_async_remote_copy(
-                    yb.at[mine], yb.at[mine], s2, r2,
-                    device_id={"tm": lax.div(i, n_sp), "space": lax.rem(i, n_sp)}, device_id_type=MESH,
-                ).start()
-
-            return carry
-
-        lax.fori_loop(0, side, gather, 0, unroll=side <= 32)
-        wait_bytes(yb.at[pl.ds(0, (len(owners) - 1) * upo)], r2)
-
-    @pl.when(jnp.logical_not(owner))
+    kinds_of = sorted({size for _, _, _, size in owners})
+    holds = [
+        (size, functools.reduce(jnp.logical_or, [m for m, o in zip(is_own, owners) if o[3] == size]))
+        for size in kinds_of
+    ]
+    begin = sum(jnp.where(m, o[2], 0) for m, o in zip(is_own, owners))
+    other = jnp.logical_not(functools.reduce(jnp.logical_or, is_own))
+    for size, flag in holds:
+
+        @pl.when(flag)
+        def _():
+            mine = pl.ds(begin, size)
+            plane[here, 0:size] = xb[mine]
+            wait_bytes(plane.at[pl.ds(0, side - 1), pl.ds(0, size)], r1)
+            yb[mine] = jnp.sum(plane[:, 0:size].astype(F32), axis=0).astype(BF)
+
+            def gather(i, carry):
+                @pl.when(i != tm * n_sp + sp)
+                def _():
+                    pltpu.make_async_remote_copy(
+                        yb.at[mine], yb.at[mine], s2, r2,
+                        device_id={"tm": lax.div(i, n_sp), "space": lax.rem(i, n_sp)},
+                        device_id_type=MESH,
+                    ).start()
+
+                return carry
+
+            lax.fori_loop(0, side, gather, 0, unroll=side <= 32)
+            wait_bytes(yb.at[pl.ds(0, units - size)], r2)
+
+    @pl.when(other)
     def _():
         wait_bytes(yb, r2)
 
     y_out[...] = yb[...]
     for ci in range(len(chunks)):
         wait_bytes(recs[ci].at[pl.ds(0, n_tm - 1)], a_send.at[ci])
-
-    @pl.when(owner)
-    def _():
-        wait_bytes(xb.at[pl.ds(0, (len(owners) - 1) * upo)], s1)
-        wait_bytes(plane.at[pl.ds(0, side - 1)], s2)
-
-    @pl.when(jnp.logical_not(owner))
+    for size, flag in holds:
+
+        @pl.when(flag)
+        def _():
+            wait_bytes(xb.at[pl.ds(0, units - size)], s1)
+            wait_bytes(plane.at[pl.ds(0, side - 1), pl.ds(0, size)], s2)
+
+    @pl.when(other)
     def _():
         wait_bytes(xb, s1)
 
@@ -310,7 +350,18 @@
     lane = lax.broadcasted_iota(jnp.int32, (modes, lanes), 1)
     lane_b = lane[:blocks]
 
-    copies, tiles = [], [yb[g].astype(F32) for g in range(groups)]
+    width = tail_width(freqs, blocks, modes)
+    per = modes // blocks
+    units = [yb[at].astype(F32) for at in range(yb.shape[0])]
+    whole = groups - 1 if width else groups
+    tiles = [jnp.concatenate(units[g * per : (g + 1) * per], axis=0) for g in range(whole)]
+    grams = units[whole * per : whole * per + whole]
+    if width:
+        cuts = [pltpu.roll(units[-1], lanes - i * width, 1) if i else units[-1] for i in range(1 + per)]
+        cuts = [jnp.where(lane_b < width, c, 0.0) for c in cuts]
+        grams.append(cuts[0])
+        tiles.append(jnp.concatenate(cuts[1:], axis=0))
+    copies = []
     row_b = lax.broadcasted_iota(jnp.int32, (blocks, modes, lanes), 0)
     pick = row_b == lax.broadcasted_iota(jnp.int32, (blocks, modes, lanes), 2) % blocks
     picked = [
@@ -343,7 +394,7 @@
             return jnp.where(freq_mask(nf, rows, lanes, blocks), big, 0.0).reshape(nf * rows, lanes)
 
         coef = tiles[g]
-        gram = yb[groups + g // 2].astype(F32)[g % 2 * blocks : (g % 2 + 1) * blocks]
+        gram = grams[g]
         vec = spread(jnp.where(lane < half, coef, -coef))
         turned = swap_halves(gram, half)
         quad = jnp.concatenate([spread(gram), spread(jnp.where(lane_b < half, -turned, turned))], axis=0)
@@ -351,10 +402,10 @@
         energy = jnp.sum(vec * mm(rows[0], quad.astype(BF), ((1,), (0,))), axis=1, keepdims=True)
         factor = 1.0 / jnp.sqrt(energy / entries + 1e-06)
         both = jnp.concatenate(rows, axis=0)
-        whole = mm(both, sh[g * lanes : g * lanes + 2 * half], ((1,), (0,)))
+        fields = mm(both, sh[g * lanes : g * lanes + 2 * half], ((1,), (0,)))
         for v in range(nvar):
             for c in range(2):
-                val = (whole[c * nf * modes : (c + 1) * nf * modes, v * pts : (v + 1) * pts] * factor).astype(BF)
+                val = (fields[c * nf * modes : (c + 1) * nf * modes, v * pts : (v + 1) * pts] * factor).astype(BF)
                 ob[c, f0 : f0 + nf, v] = val.reshape(nf, modes, pts)
         cp = pltpu.make_async_copy(ob.at[:, pl.ds(f0, nf)], new_out.at[:, pl.ds(f0, nf)], o_sem.at[g])
         cp.start()
@@ -374,12 +425,11 @@
         blocks = offsets.shape[0]
         groups = -(-freqs // GROUP)
         entries = nvar * pts * n
-        pairs = groups + -(-groups // 2)
         side = n_tm * n_sp
-        upo = -(-pairs // side)
-        owners = owner_list(n_tm, n_sp, -(-pairs // upo))
+        units = unit_count(freqs, blocks, modes)
+        owners = owner_list(n_tm, n_sp, units)
         table_rows = 2 * freqs * blocks
-        unit = (2 * blocks, 2 * GROUP * blocks)
+        unit = (blocks, 2 * GROUP * blocks)
         chunks = tuple((v, min(v + 2, nvar)) for v in range(0, nvar, 2))
         snap = jnp.transpose(snapshots, (1, 0, 2))
         base = jnp.transpose(basis, (0, 1, 3, 2, 4))
@@ -389,16 +439,16 @@
             functools.partial(kernel, n_tm, n_sp, owners, entries, chunks),
             out_shape=(
                 jax.ShapeDtypeStruct((table_rows, nvar * pts), BF),
-                jax.ShapeDtypeStruct((len(owners) * upo,) + unit, BF),
+                jax.ShapeDtypeStruct((units,) + unit, BF),
             ),
             in_specs=[hbm] * 5,
             out_specs=(vmem, vmem),
             scratch_shapes=[
                 pltpu.VMEM((table_rows, rows * n_tm), BF),
                 pltpu.VMEM((2, freqs, nvar, modes, pts), BF),
-                pltpu.VMEM((len(owners) * upo,) + unit, BF),
-                pltpu.VMEM((side, upo) + unit, BF),
-                pltpu.VMEM((len(owners) * upo,) + unit, BF),
+                pltpu.VMEM((units,) + unit, BF),
+                pltpu.VMEM((side, max(o[3] for o in owners)) + unit, BF),
+                pltpu.VMEM((units,) + unit, BF),
                 pltpu.VMEM(mass_table.shape, F32),
                 pltpu.SMEM(elem_kind.shape, jnp.int32),
                 pltpu.SMEM(offsets.shape, jnp.int32),
@@ -408,7 +458,7 @@
                 pltpu.SemaphoreType.DMA((len(chunks),)),
                 pltpu.SemaphoreType.DMA((len(chunks),)),
                 pltpu.SemaphoreType.DMA((4,)),
-                pltpu.SemaphoreType.REGULAR((3,)),
+                pltpu.SemaphoreType.REGULAR((4,)),
             ]
             + [pltpu.SemaphoreType.DMA] * 4,
             compiler_params=pltpu.CompilerParams(

time: 32.1 us -> 31.7 us (0.988)
  Pallas kernels: 31.3 us -> 30.9 us
    pallas_call x1, Pallas kernels: 29.9 us -> 29.4 us  [on_device(): pl.pallas_call(functools.partial(kernel, n_tm, n_sp, owners, entries, chu...]
where the time goes in v6:
time: 31.7 us; the launch traced here: 31.5 us
  Pallas kernels  30.9 us (97%)
  between operations  0.64 us (2%)
    pallas_call x1, Pallas kernels, on_device(): pl.pallas_call(functools.partial(kernel, n_tm, n_sp, owners, entries, chu...  29.4 us
    pallas_call x1, Pallas kernels, on_device(): pl.pallas_call(functools.partial(finish, entries), out_shape=(jax.ShapeDt...  1.51 us

profile of v6, /device:TPU:0, one launch (start us, length us, event | category | flops | bytes accessed | tf_op | source)
XLA Modules:
  0.0 31.5 jit_solution(15571879648047408860)
XLA Ops:
  0.6 29.4 %shard_map.68 = (bf16[528,640]{1,0:T(8,128)(2,1)S(1)}, bf16[13,8,128]{2,1,0:T(8,128)(2,1)S(1)}) custom-call(bf16[5,32,2048]{2,1,0:T(8,128)(2,1)} %bitcast.5, bf16[2,33,5,16,128]{4,3,2,1,0:T(8,128)(2,1)} %bitcast.4, f32[8,64,64]{2,1,0:T(8,128)} %mass_in.1, s32[2]{0:T(128)} %kinds_in.1, s32[8]{0:T(128)} %offs_in.1), custom_call_target="tpu_custom_call" | custom-call | tf_op jit(solution)/shard_map/pallas_call | solution.py:438
  30.0 1.5 %shard_map.69 = (f32[2,8,16,33]{3,2,1,0:T(8,128)}, bf16[2,33,5,16,128]{4,3,2,1,0:T(8,128)(2,1)}) custom-call(bf16[13,8,128]{2,1,0:T(8,128)(2,1)S(1)} %get-tuple-element.6.yb, bf16[528,640]{1,0:T(8,128)(2,1)S(1)} %get-tuple-element.7.sh), custom_call_target="tpu_custom_call" | custom-call | tf_op jit(solution)/shard_map/pallas_call | solution.py:468

commit v7 on v6

--- a/solution.py
+++ b/solution.py
@@ -134,7 +134,7 @@
         v0, v1 = chunks[ci]
 
         def send(i, carry):
-            to = to_lev * quart + lax.rem(place + i, quart)
+            to = to_lev * quart + (lax.rem(place + i, quart) if first else quart - 1 - i)
             pltpu.make_async_remote_copy(
                 snap.at[pl.ds(v0, v1 - v0), :, pl.ds(pl.multiple_of(to * pts, pts), pts)],
                 recs[ci].at[tm], a_send.at[ci], a_recv.at[ci],
@@ -233,7 +233,7 @@
         pltpu.make_async_copy(rec, rec, a_recv.at[ci]).wait()
         count = v1 - v0
         x = jnp.concatenate([rec[:, v].reshape(record, pts) for v in range(count)], axis=1)
-        cuts = [0, table.shape[0]] if count > 1 else [0, lanes * (groups // 2), table.shape[0]]
+        cuts = [0, table.shape[0]] if count > 1 else [0, lanes, 2 * lanes, 3 * lanes, table.shape[0]]
         spec = jnp.concatenate([mm(table[i:j], x, ((1,), (0,))) for i, j in zip(cuts, cuts[1:])], axis=0)
         s_hi = spec.astype(BF)
         s_lo = (spec - s_hi.astype(F32)).astype(BF)

time: 31.7 us -> 31.6 us (level)
  no operation moved by 1% of the time
where the time goes in v7:
time: 31.6 us; the launch traced here: 31.4 us
  Pallas kernels  30.8 us (97%)
  between operations  0.64 us (2%)
    pallas_call x1, Pallas kernels, on_device(): pl.pallas_call(functools.partial(kernel, n_tm, n_sp, owners, entries, chu...  29.2 us
    pallas_call x1, Pallas kernels, on_device(): pl.pallas_call(functools.partial(finish, entries), out_shape=(jax.ShapeDt...  1.51 us

profile of v7, /device:TPU:0, one launch (start us, length us, event | category | flops | bytes accessed | tf_op | source)
XLA Modules:
  0.0 31.4 jit_solution(9581188065610918117)
XLA Ops:
  0.6 29.2 %shard_map.68 = (bf16[528,640]{1,0:T(8,128)(2,1)S(1)}, bf16[13,8,128]{2,1,0:T(8,128)(2,1)S(1)}) custom-call(bf16[5,32,2048]{2,1,0:T(8,128)(2,1)} %bitcast.5, bf16[2,33,5,16,128]{4,3,2,1,0:T(8,128)(2,1)} %bitcast.4, f32[8,64,64]{2,1,0:T(8,128)} %mass_in.1, s32[2]{0:T(128)} %kinds_in.1, s32[8]{0:T(128)} %offs_in.1), custom_call_target="tpu_custom_call" | custom-call | tf_op jit(solution)/shard_map/pallas_call | solution.py:438
  29.9 1.5 %shard_map.69 = (f32[2,8,16,33]{3,2,1,0:T(8,128)}, bf16[2,33,5,16,128]{4,3,2,1,0:T(8,128)(2,1)}) custom-call(bf16[13,8,128]{2,1,0:T(8,128)(2,1)S(1)} %get-tuple-element.6.yb, bf16[528,640]{1,0:T(8,128)(2,1)S(1)} %get-tuple-element.7.sh), custom_call_target="tpu_custom_call" | custom-call | tf_op jit(solution)/shard_map/pallas_call | solution.py:468

commit v8 on v7

--- a/solution.py
+++ b/solution.py
@@ -430,7 +430,7 @@
         owners = owner_list(n_tm, n_sp, units)
         table_rows = 2 * freqs * blocks
         unit = (blocks, 2 * GROUP * blocks)
-        chunks = tuple((v, min(v + 2, nvar)) for v in range(0, nvar, 2))
+        chunks = ((0, min(2, nvar)),) + tuple((v, v + 1) for v in range(2, nvar))
         snap = jnp.transpose(snapshots, (1, 0, 2))
         base = jnp.transpose(basis, (0, 1, 3, 2, 4))
         hbm = pl.BlockSpec(memory_space=pltpu.HBM)

time: 31.6 us -> 31.6 us (level)
  no operation moved by 1% of the time
where the time goes in v8:
time: 31.6 us; the launch traced here: 31.4 us
  Pallas kernels  30.8 us (97%)
  between operations  0.64 us (2%)
    pallas_call x1, Pallas kernels, on_device(): pl.pallas_call(functools.partial(kernel, n_tm, n_sp, owners, entries, chu...  29.3 us
    pallas_call x1, Pallas kernels, on_device(): pl.pallas_call(functools.partial(finish, entries), out_shape=(jax.ShapeDt...  1.51 us

profile of v8, /device:TPU:0, one launch (start us, length us, event | category | flops | bytes accessed | tf_op | source)
XLA Modules:
  0.0 31.4 jit_solution(6761713884322570440)
XLA Ops:
  0.6 29.3 %shard_map.68 = (bf16[528,640]{1,0:T(8,128)(2,1)S(1)}, bf16[13,8,128]{2,1,0:T(8,128)(2,1)S(1)}) custom-call(bf16[5,32,2048]{2,1,0:T(8,128)(2,1)} %bitcast.5, bf16[2,33,5,16,128]{4,3,2,1,0:T(8,128)(2,1)} %bitcast.4, f32[8,64,64]{2,1,0:T(8,128)} %mass_in.1, s32[2]{0:T(128)} %kinds_in.1, s32[8]{0:T(128)} %offs_in.1), custom_call_target="tpu_custom_call" | custom-call | tf_op jit(solution)/shard_map/pallas_call | solution.py:438
  29.9 1.5 %shard_map.69 = (f32[2,8,16,33]{3,2,1,0:T(8,128)}, bf16[2,33,5,16,128]{4,3,2,1,0:T(8,128)(2,1)}) custom-call(bf16[13,8,128]{2,1,0:T(8,128)(2,1)S(1)} %get-tuple-element.6.yb, bf16[528,640]{1,0:T(8,128)(2,1)S(1)} %get-tuple-element.7.sh), custom_call_target="tpu_custom_call" | custom-call | tf_op jit(solution)/shard_map/pallas_call | solution.py:468

commit v9 on v8

--- a/solution.py
+++ b/solution.py
@@ -58,8 +58,8 @@
 def kernel(
     n_tm, n_sp, owners, entries, chunks,
     snap, basis, mass_in, kinds_in, offs_in,
-    sh, y_out,
-    table, ub, xb, plane, yb, mass, kinds, offs, *rest,
+    sh, yb,
+    table, ub, xb, plane, mass, kinds, offs, *rest,
 ):
     recs, (a_send, a_recv, l_sem, known, s1, r1, s2, r2) = rest[: len(chunks)], rest[len(chunks) :]
     tm = lax.axis_index("tm")
@@ -327,7 +327,6 @@
     def _():
         wait_bytes(yb, r2)
 
-    y_out[...] = yb[...]
     for ci in range(len(chunks)):
         wait_bytes(recs[ci].at[pl.ds(0, n_tm - 1)], a_send.at[ci])
     for size, flag in holds:
@@ -448,7 +447,6 @@
                 pltpu.VMEM((2, freqs, nvar, modes, pts), BF),
                 pltpu.VMEM((units,) + unit, BF),
                 pltpu.VMEM((side, max(o[3] for o in owners)) + unit, BF),
-                pltpu.VMEM((units,) + unit, BF),
                 pltpu.VMEM(mass_table.shape, F32),
                 pltpu.SMEM(elem_kind.shape, jnp.int32),
                 pltpu.SMEM(offsets.shape, jnp.int32),

time: 31.6 us -> 31.6 us (level)
  no operation moved by 1% of the time
where the time goes in v9:
time: 31.6 us; the launch traced here: 31.4 us
  Pallas kernels  30.8 us (97%)
  between operations  0.64 us (2%)
    pallas_call x1, Pallas kernels, on_device(): pl.pallas_call(functools.partial(kernel, n_tm, n_sp, owners, entries, chu...  29.2 us
    pallas_call x1, Pallas kernels, on_device(): pl.pallas_call(functools.partial(finish, entries), out_shape=(jax.ShapeDt...  1.51 us

profile of v9, /device:TPU:0, one launch (start us, length us, event | category | flops | bytes accessed | tf_op | source)
XLA Modules:
  0.0 31.4 jit_solution(1045757161554911141)
XLA Ops:
  0.6 29.2 %shard_map.68 = (bf16[528,640]{1,0:T(8,128)(2,1)S(1)}, bf16[13,8,128]{2,1,0:T(8,128)(2,1)S(1)}) custom-call(bf16[5,32,2048]{2,1,0:T(8,128)(2,1)} %bitcast.5, bf16[2,33,5,16,128]{4,3,2,1,0:T(8,128)(2,1)} %bitcast.4, f32[8,64,64]{2,1,0:T(8,128)} %mass_in.1, s32[2]{0:T(128)} %kinds_in.1, s32[8]{0:T(128)} %offs_in.1), custom_call_target="tpu_custom_call" | custom-call | tf_op jit(solution)/shard_map/pallas_call | solution.py:437
  29.9 1.5 %shard_map.69 = (f32[2,8,16,33]{3,2,1,0:T(8,128)}, bf16[2,33,5,16,128]{4,3,2,1,0:T(8,128)(2,1)}) custom-call(bf16[13,8,128]{2,1,0:T(8,128)(2,1)S(1)} %get-tuple-element.6.yb, bf16[528,640]{1,0:T(8,128)(2,1)S(1)} %get-tuple-element.7.sh), custom_call_target="tpu_custom_call" | custom-call | tf_op jit(solution)/shard_map/pallas_call | solution.py:466
